TPU v7x, 128 devices: a whole 4x4x4 slice. The times are simulated.
128 devices in a mesh: grp: 4 (over y), sfc: 32 (over z, x, core).
Axes of the slice: x: 4, y: 4, z: 4, core: 2. Of those that a mesh axis runs over, the one named last changes fastest.
Arguments:
- flow_fields: float32 [4, 5, 8192, 128], P('grp', None, 'sfc'), may hold values from -6 to 6
- mean_velocity: float32 [4, 3, 8192, 128], P('grp', None, 'sfc'), may hold values from -3 to 3
- cell_eddy_viscosity: float32 [4, 8192, 128], P('grp', 'sfc'), may hold values from 0.01 to 0.08
- tile_links: int32 [4, 4, 8192], P('grp', None, 'sfc'), may hold values from -1 to 8191, as said below
- tile_target: int32 [4, 8192], P('grp', 'sfc'), may hold values from 0 to 8191, as said below
- projector: float32 [64, 128], replicated, may hold values from -0.5 to 0.5
- acoustic_state: float32 [4, 4, 64, 8192], P('grp', None, None, 'sfc'), may hold values from -6 to 6
- element_face_neighbours: int32 [4, 6, 8192], P('grp', None, 'sfc'), may hold values from -1 to 8191, as said below
- face_codes: int32 [4, 6, 8192], P('grp', None, 'sfc'), may hold values from 0 to 3
Outputs:
- flow_out: float32 [4, 5, 8192, 128], P('grp', None, 'sfc')
- mean_velocity_output: float32 [4, 3, 8192, 128], P('grp', None, 'sfc')
- acoustic_out: float32 [4, 4, 64, 8192], P('grp', None, None, 'sfc')
Inputs may be any that keep to these rules, and one draw needn't show every extreme that they name: `tile_links`: each entry is -1 or a tile of the same grp index whose position differs from the tile's own by at most 16. `tile_target`: element e lies on acoustic device e // 256. A tile held at sfc index s targets an element of acoustic device s or s + 1; one flow device sends at most 160 tiles to device s + 1, and in every draw some flow device sends exactly 160. Entries of grp index 3 are not read. `element_face_neighbours`: each entry is -1 or an element whose index differs from the element's own by at most 16.
All inputs are finite; a program needn't handle non-finite values.
Results may differ from a plain program's by a relative error of at most 0.0008.
Values may be sent and summed in bfloat16 or wider, within the bound.
A program may use at most 128 MiB of HBM per device.

v0:
```python
import jax
import jax.numpy as jnp
import numpy as np
from jax import lax
from jax.sharding import PartitionSpec as P

HW = 16
HE = 16
CAP = 160


ADVECT = 0.1
RELAX = 0.1
PENALTY = 1.5
ACOUSTIC_STEP = 0.08


def for_sending(x):

    def short(part):
        return part.astype(jnp.bfloat16) if part.dtype == jnp.float32 else part

    return jax.tree.map(short, x)


def with_halo(x, sides, width):
    for axis, dim in sides:
        count, length = (lax.axis_size(axis), x.shape[dim])
        up = [(i, (i + 1) % count) for i in range(count - 1)]
        down = [(j, i) for i, j in up]
        last = lax.slice_in_dim(x, length - width, length, axis=dim)
        first = lax.slice_in_dim(x, 0, width, axis=dim)
        before = lax.ppermute(last, axis, up)
        after = lax.ppermute(first, axis, down)
        x = jnp.concatenate([before, x, after], axis=dim)
    return x


def copy_for_each(x, axis):
    count = lax.axis_size(axis)
    return lax.all_to_all(jnp.broadcast_to(x[None], (count, *x.shape)), axis, 0, 0, tiled=True)


def joined_along(blocks, dim):
    blocks = jnp.moveaxis(blocks, 0, dim)
    shape = blocks.shape
    return blocks.reshape(*shape[:dim], shape[dim] * shape[dim + 1], *shape[dim + 2 :])


def gathered_copies(x, axis, dim):
    blocks = copy_for_each(x, axis)
    return joined_along(blocks, dim)


def in_one_piece(arrays, axis, dim, along):
    both = jnp.concatenate(arrays, axis=along)
    filled, at, gathered = (gathered_copies(both, axis, dim), 0, [])
    for a in arrays:
        gathered.append(lax.slice_in_dim(filled, at, at + a.shape[along], axis=along))
        at += a.shape[along]
    return tuple(gathered)


def shifted(value, axis, steps):
    count = lax.axis_size(axis)
    first, last = (max(0, -steps), min(count, count - steps))
    return lax.ppermute(value, axis, [(source, source + steps) for source in range(first, last)])


def derivative_operators():
    points = np.array([-1.0, -1.0 / np.sqrt(5.0), 1.0 / np.sqrt(5.0), 1.0])
    weights = np.array(
        [
            1.0 / np.prod([points[col] - points[other] for other in range(4) if other != col])
            for col in range(4)
        ]
    )
    derivative_matrix = np.zeros((4, 4))
    for line in range(4):
        for col in range(4):
            if line != col:
                derivative_matrix[line, col] = (
                    weights[col] / weights[line] / (points[line] - points[col])
                )
        derivative_matrix[line, line] = -derivative_matrix[line].sum()
    identity = np.eye(4)
    return np.stack(
        [
            np.kron(identity, np.kron(identity, derivative_matrix)),
            np.kron(identity, np.kron(derivative_matrix, identity)),
            np.kron(derivative_matrix, np.kron(identity, identity)),
        ]
    ).astype(np.float32)


def near_take(field, links, dimension):
    return jnp.take(field, links, axis=dimension)


def flow_advance(solver_state, anchor, links, viscosity):
    amount_rows = links.shape[1]
    center = lax.slice_in_dim(solver_state, anchor, anchor + amount_rows, axis=1)
    north = near_take(solver_state, links[0], 1)
    south = near_take(solver_state, links[1], 1)
    upper = near_take(solver_state, links[2], 1)
    lower = near_take(solver_state, links[3], 1)
    east = jnp.roll(center, -1, axis=2)
    west = jnp.roll(center, 1, axis=2)
    laplace = east + west + north + south + upper + lower - 6.0 * center
    advection = (
        center[1] * (east - west) * 0.5
        + center[2] * (north - south) * 0.5
        + center[3] * (upper - lower) * 0.5
    )
    return center + viscosity * laplace - ADVECT * advection


def lamb_vector(solver_state, anchor, links):
    velocity = solver_state[1:4]
    amount_rows = links.shape[1]
    center = lax.slice_in_dim(velocity, anchor, anchor + amount_rows, axis=1)
    east = jnp.roll(center, -1, axis=2)
    west = jnp.roll(center, 1, axis=2)
    along_x = (east - west) * 0.5
    along_y = (near_take(velocity, links[0], 1) - near_take(velocity, links[1], 1)) * 0.5
    along_z = (near_take(velocity, links[2], 1) - near_take(velocity, links[3], 1)) * 0.5
    vort_x = along_y[2] - along_z[1]
    vort_y = along_z[0] - along_x[2]
    vort_z = along_x[1] - along_y[0]
    return jnp.stack(
        [
            vort_y * center[2] - vort_z * center[1],
            vort_z * center[0] - vort_x * center[2],
            vort_x * center[1] - vort_y * center[0],
        ]
    )


def project(lamb, average, projector):
    packed = jnp.concatenate([lamb, average], 0)
    mapped = jnp.einsum("ctm,nm->tcn", packed, projector, precision=lax.Precision.HIGHEST)
    return mapped.reshape(mapped.shape[0], -1).astype(jnp.bfloat16)


def face_view(grid, face):
    axis_id = face // 2
    level = 3 * (face % 2)
    if axis_id == 0:
        return grid[:, :, :, level]
    if axis_id == 1:
        return grid[:, :, level, :]
    return grid[:, level]


def face_added(grid, face, update):
    axis_id = face // 2
    level = 3 * (face % 2)
    if axis_id == 0:
        return grid.at[:, :, :, level].add(update)
    if axis_id == 1:
        return grid.at[:, :, level, :].add(update)
    return grid.at[:, level].add(update)


def turned_face(remote, turn):
    if turn == 0:
        return remote
    if turn == 1:
        return jnp.swapaxes(jnp.flip(remote, 2), 1, 2)
    if turn == 2:
        return jnp.flip(remote, (1, 2))
    return jnp.swapaxes(jnp.flip(remote, 1), 1, 2)


def acoustic_advance(solver_state, wide, links, valid, codes, source):
    derivative_matrix = jnp.asarray(derivative_operators())
    gradient_fields = jnp.einsum(
        "yws,lsb->ylwb", derivative_matrix, solver_state, precision=lax.Precision.HIGHEST
    )
    lamb_src = source[0:3]
    mean_flow = source[3:6]
    convect = (
        mean_flow[0][None] * gradient_fields[0]
        + mean_flow[1][None] * gradient_fields[1]
        + mean_flow[2][None] * gradient_fields[2]
    )
    rhs_parts = [
        -(gradient_fields[0, 1] + gradient_fields[1, 2] + gradient_fields[2, 3]) - convect[0]
    ]
    for direction in range(3):
        rhs_parts.append(
            -gradient_fields[direction, 0] - convect[1 + direction] - lamb_src[direction]
        )
    elements = solver_state.shape[2]
    rhs_grid = jnp.stack(rhs_parts).reshape(4, 4, 4, 4, elements)
    state_grid = solver_state.reshape(4, 4, 4, 4, elements)
    wide_grid = wide.reshape(4, 4, 4, 4, wide.shape[2])
    for face in range(6):
        facing = face_view(wide_grid, face ^ 1)
        remote = near_take(facing, links[face], 3)
        turned = None
        for turn in range(4):
            term = jnp.where(
                codes[face][None, None, None, :] == turn,
                turned_face(remote, turn),
                jnp.float32(0.0),
            )
            turned = term if turned is None else turned + term
        jump = jnp.where(
            valid[face][None, None, None, :], turned - face_view(state_grid, face), jnp.float32(0.0)
        )
        rhs_grid = face_added(rhs_grid, face, PENALTY * jump)
    return solver_state + ACOUSTIC_STEP * rhs_grid.reshape(4, 64, elements)


def gather_sources(rows, ids, count):
    index = jnp.where(ids < 0, count, ids).astype(jnp.int32)
    sums = (
        jnp.zeros((count + 1, rows.shape[1]), jnp.float32).at[index].add(rows.astype(jnp.float32))
    )
    counts = (
        jnp.zeros((count + 1,), jnp.float32)
        .at[index]
        .add(jnp.where(ids < 0, jnp.float32(0.0), jnp.float32(1.0)))
    )
    source = sums[:count] / jnp.maximum(counts[:count], 1.0)[:, None]
    return jnp.transpose(source.reshape(count, 6, -1), (1, 2, 0))


def localize(global_links, own_global, base, extent):
    resolved = jnp.where(global_links < 0, own_global[None, :], global_links)
    return jnp.clip(resolved - base, 0, extent - 1)


def widen_trace(field):
    return with_halo(for_sending(field), (("sfc", 2),), HE).astype(field.dtype)


def body(
    flow_fields,
    mean_velocity,
    cell_eddy_viscosity,
    tile_links,
    tile_target,
    projector,
    acoustic_state,
    element_face_neighbours,
    face_codes,
):
    groups = lax.axis_size("grp")
    group_index = lax.axis_index("grp")
    column = lax.axis_index("sfc")
    is_flow = group_index < groups - 1
    solver_state = flow_fields[0]
    average = mean_velocity[0]
    viscosity = cell_eddy_viscosity[0]
    global_links = tile_links[0]
    tile_count = solver_state.shape[1]
    first_tile = column * tile_count
    own_global = first_tile + jnp.arange(tile_count, dtype=jnp.int32)
    payloads = []
    packed = jnp.concatenate([solver_state, viscosity[None]], 0)
    wide = with_halo(packed, (("sfc", 1),), 3 * HW)
    wide_links = with_halo(global_links, (("sfc", 1),), 2 * HW)
    field = wide[:5]
    wide_visc = wide[5]
    band = tile_count + 4 * HW
    narrow = tile_count + 2 * HW
    band_global = first_tile - 2 * HW + jnp.arange(band, dtype=jnp.int32)
    links_one = localize(wide_links, band_global, first_tile - 3 * HW, tile_count + 6 * HW)
    section_one = flow_advance(field, HW, links_one, wide_visc[HW : HW + band])
    own_links = localize(
        wide_links[:, 2 * HW : 2 * HW + tile_count], own_global, first_tile - 2 * HW, band
    )
    lamb = lamb_vector(section_one, 2 * HW, own_links)
    average = (1.0 - RELAX) * average + RELAX * section_one[1:4, 2 * HW : 2 * HW + tile_count]
    payloads.append(project(lamb, average, projector))
    narrow_global = first_tile - HW + jnp.arange(narrow, dtype=jnp.int32)
    links_two = localize(wide_links[:, HW : HW + narrow], narrow_global, first_tile - 2 * HW, band)
    section_two = flow_advance(section_one, HW, links_two, wide_visc[2 * HW : 2 * HW + narrow])
    final_links = localize(
        wide_links[:, 2 * HW : 2 * HW + tile_count], own_global, first_tile - HW, narrow
    )
    lamb = lamb_vector(section_two, HW, final_links)
    solver_state = section_two[:, HW : HW + tile_count]
    average = (1.0 - RELAX) * average + RELAX * solver_state[1:4]
    payloads.append(project(lamb, average, projector))
    elements = acoustic_state.shape[3]
    targets = tile_target[0]
    owner = targets // elements
    local = targets % elements
    is_next = is_flow & (owner != column)
    own_marks = jnp.where(is_flow & (owner == column), local + 1, 0)
    next_marks = jnp.where(is_next, local + 1, 0)
    width = payloads[0].shape[1]
    sound = acoustic_state[0]
    neighbours = element_face_neighbours[0]
    valid = neighbours >= 0
    trace_links = jnp.clip(neighbours - (column * elements - HE), 0, elements + 2 * HE - 1)
    for turn in range(2):
        got_rows, got_marks, got_next = (
            gathered_copies(payloads[turn][None], "grp", 0),
            *in_one_piece((own_marks[None], next_marks[None]), "grp", 0, 1),
        )
        flags = (got_next > 0).astype(jnp.int32)
        rank = jnp.cumsum(flags, axis=1) - flags
        row_base = (jnp.arange(groups, dtype=jnp.int32) * CAP)[:, None]
        slot = jnp.where(flags > 0, row_base + rank, groups * CAP).reshape(-1)
        passed = (
            jnp.zeros((groups * CAP, width), jnp.bfloat16)
            .at[slot]
            .set(got_rows.reshape(-1, width), mode="drop")
        )
        passed_marks = (
            jnp.zeros((groups * CAP,), jnp.int32).at[slot].set(got_next.reshape(-1), mode="drop")
        )
        moved, moved_marks = shifted((passed, passed_marks), "sfc", 1)
        rows = jnp.concatenate([got_rows.reshape(-1, width), moved], 0)
        marks = jnp.concatenate([got_marks.reshape(-1), moved_marks], 0)
        source = gather_sources(rows, marks - 1, elements)
        wide_sound = widen_trace(sound)
        sound = acoustic_advance(sound, wide_sound, trace_links, valid, face_codes[0], source)
    flow_out = jnp.where(is_flow, solver_state, flow_fields[0])[None]
    mean_velocity_output = jnp.where(is_flow, average, mean_velocity[0])[None]
    acoustic_out = jnp.where(group_index == groups - 1, sound, acoustic_state[0])[None]
    return (flow_out, mean_velocity_output, acoustic_out)


def solution(mesh):
    placed = (
        P("grp", None, "sfc", None),
        P("grp", None, "sfc", None),
        P("grp", "sfc", None),
        P("grp", None, "sfc"),
        P("grp", "sfc"),
        P(),
        P("grp", None, None, "sfc"),
        P("grp", None, "sfc"),
        P("grp", None, "sfc"),
    )
    return jax.shard_map(
        body,
        mesh=mesh,
        in_specs=placed,
        out_specs=(
            P("grp", None, "sfc", None),
            P("grp", None, "sfc", None),
            P("grp", None, None, "sfc"),
        ),
        check_vma=False,
    )
```

profile of v0, /device:TPU:47, one launch (start us, length us, event | category | flops | bytes accessed | tf_op | source)
XLA Modules:
  0.0 341.5 jit_solution(4735734955226965109)
XLA Ops:
  1.5 4.0 %collective-permute-start.2 = (s32[4,32]{1,0:T(4,128)S(1)}, s32[4,32]{1,0:T(4,128)S(1)}, u32[]{:S(2)}, u32[]{:S(2)}) collective-permute-start(s32[4,32]{1,0:T(4,128)S(1)} %get-tuple-element.340), channel_id=1, source_target_pairs={{0,1},{1,2},{2,3},{3,4},{4,5},{5,6},{6,7},{7,8},{8,9},{9,10},{10,1... | collective-permute-start | bytes 1544 | tf_op jit(solution)/shard_map/ppermute | solution.py:33
  9.2 5.7 %collective-permute-start = (f32[6,48,128]{2,1,0:T(8,128)}, f32[6,48,128]{2,1,0:T(8,128)}, u32[]{:S(2)}, u32[]{:S(2)}) collective-permute-start(f32[6,48,128]{2,1,0:T(8,128)} %get-tuple-element.273), channel_id=1, source_target_pairs={{0,1},{1,2},{2,3},{3,4},{4,5},{5,6},{6,7},{7,8},{8,9},{9,10},{10,1... | collective-permute-start | bytes 442376 | tf_op jit(solution)/shard_map/ppermute | solution.py:33
  18.2 4.3 %all-to-all-start = ((s32[4,1,512]{2,1,0:T(1,128)}), s32[4,1,512]{2,1,0:T(1,128)S(1)}, u32[]{:S(2)}, u32[]{:S(2)}) async-start(s32[4,1,512]{2,1,0:T(1,128)} %broadcast_in_dim.469), calls=%async_computation | async-start | bytes 16384 | tf_op jit(solution)/shard_map/all_to_all | solution.py:41
  23.6 6.3 %collective-permute-start.6 = (bf16[4,64,16]{2,1,0:T(8,128)(2,1)S(1)}, bf16[4,64,16]{2,1,0:T(8,128)(2,1)S(1)}, u32[]{:S(2)}, u32[]{:S(2)}) collective-permute-start(bf16[4,64,16]{2,1,0:T(8,128)(2,1)S(1)} %get-tuple-element.308), channel_id=1, source_target_pairs={{0,1},{1,2},{2,3},{3,4},{4,5},{5,6},{6,7},{7,8},{8,9},{9,10},{10,1... | collective-permute-start | bytes 24584 | tf_op jit(solution)/shard_map/ppermute | solution.py:33
  53.8 4.9 %scatter_custom_fusion = s32[640]{0:T(1024)} fusion(s32[1024]{0:T(1024)S(1)} %bitcast.728, s32[1024]{0:T(1024)S(1)} %bitcast.731, s32[]{:T(128)} %constant.410.clone.1), kind=kCustom, calls=%fused_computation.502 | custom fusion | bytes 2564 | tf_op jit(solution)/shard_map/scatter | solution.py:315
  58.7 5.7 %collective-permute-start.4 = (s32[640]{0:T(1024)}, s32[640]{0:T(1024)}, u32[]{:S(2)}, u32[]{:S(2)}) collective-permute-start(s32[640]{0:T(1024)} %scatter_custom_fusion), channel_id=1, source_target_pairs={{0,1},{1,2},{2,3},{3,4},{4,5},{5,6},{6,7},{7,8},{8,9},{9,10},{10,1... | collective-permute-start | bytes 7688 | tf_op jit(solution)/shard_map/ppermute | solution.py:67
  67.2 3.4 gather_fusion.13
  74.9 3.4 gather_fusion.14
  81.6 3.4 gather_fusion.12
  90.0 3.4 gather_fusion.15
  93.3 2.5 copy.2745
  96.8 3.4 gather_fusion.16
  103.9 3.4 gather_fusion.17
  129.1 4.4 %fusion.13 = f32[5,320,128]{2,1,0:T(8,128)S(1)} fusion(f32[320,5,128]{2,1,0:T(8,128)} %gather_fusion.3, f32[320,5,128]{2,1,0:T(8,128)} %gather_fusion.2, f32[320,5,128]{2,1,0:T(8,128)} %gather_fusion.1, f32[320,5,128]{2,1,0:T(8,128)} %gather_fusion, f32[6,352,128]{2,1,0:T(8,128)S(1)} %pad_maximum_fusion, f32[5,320,127]{2,1,0:T(8,128)} %get-tuple-element.257, ...), kind=kLoop, calls=%fused_computation.56 | loop fusion | flops 5120000 | bytes 7210240 | tf_op jit(solution)/shard_map/sub | solution.py:115
  147.7 4.4 %fusion.36 = f32[5,288,128]{2,1,0:T(8,128)S(1)} fusion(f32[288,5,128]{2,1,0:T(8,128)} %gather_fusion.7, f32[288,5,128]{2,1,0:T(8,128)} %gather_fusion.6, f32[288,5,128]{2,1,0:T(8,128)} %gather_fusion.5, f32[288,5,128]{2,1,0:T(8,128)} %gather_fusion.4, f32[5,320,128]{2,1,0:T(8,128)S(1)} %fusion.13, f32[5,288,127]{2,1,0:T(8,128)} %get-tuple-element.270, ...), kind=kLoop, calls=%fused_computation.91 | loop fusion | flops 4608000 | bytes 6489216 | tf_op jit(solution)/shard_map/sub | solution.py:115
  167.8 4.3 %all-to-all-start.2 = ((bf16[4,1,256,384]{3,2,1,0:T(8,128)(2,1)}), bf16[4,1,256,384]{3,2,1,0:T(8,128)(2,1)S(1)}, u32[]{:S(2)}, u32[]{:S(2)}) async-start(bf16[4,1,256,384]{3,2,1,0:T(8,128)(2,1)} %broadcast_in_dim.513), calls=%async_computation.2 | async-start | bytes 1572864 | tf_op jit(solution)/shard_map/all_to_all | solution.py:41
  183.6 4.4 %all-to-all-start.1 = ((bf16[4,1,256,384]{3,2,1,0:T(8,128)(2,1)}), bf16[4,1,256,384]{3,2,1,0:T(8,128)(2,1)}, u32[]{:S(2)}, u32[]{:S(2)}) async-start(bf16[4,1,256,384]{3,2,1,0:T(8,128)(2,1)} %broadcast_in_dim.473), calls=%async_computation.1 | async-start | bytes 1572864 | tf_op jit(solution)/shard_map/all_to_all | solution.py:41
  192.1 12.7 %scatter_custom_fusion.3 = f32[257]{0:T(512)S(1)} fusion(s32[1664]{0:T(1024)S(1)} %fusion.151, f32[1664]{0:T(1024)S(1)} %fusion.150, f32[]{:T(128)} %constant.422.clone.1), kind=kCustom, calls=%fused_computation.538 | custom fusion | flops 1664 | bytes 1032 | tf_op jit(solution)/shard_map/scatter-add | solution.py:224
  204.8 6.0 %scatter_custom_fusion.4 = bf16[640,384]{1,0:T(8,128)(2,1)} fusion(s32[1024]{0:T(1024)} %bitcast.729, bf16[1024,384]{1,0:T(8,128)(2,1)S(1)} %bitcast.674, bf16[]{:T(256)} %constant.431.clone.1), kind=kCustom, calls=%fused_computation.159 | custom fusion | bytes 492032 | tf_op jit(solution)/shard_map/scatter | solution.py:312
  210.8 3.0 collective-permute-start.8
  213.8 6.2 %scatter_custom_fusion.1 = bf16[640,384]{1,0:T(8,128)(2,1)} fusion(s32[1024]{0:T(1024)} %bitcast.730, bf16[1024,384]{1,0:T(8,128)(2,1)} %bitcast.41, bf16[]{:T(256)} %constant.431.clone.1), kind=kCustom, calls=%fused_computation.161 | custom fusion | bytes 492032 | tf_op jit(solution)/shard_map/scatter | solution.py:312
  223.4 15.5 %scatter_custom_fusion.5 = f32[257,384]{1,0:T(8,128)S(1)} fusion(s32[1664]{0:T(1024)S(1)} %fusion.151, bf16[640,384]{1,0:T(8,128)(2,1)S(1)} %collective-permute-done.8, bf16[]{:T(256)} %constant.487, bf16[1024,384]{1,0:T(8,128)(2,1)S(1)} %bitcast.675, f32[]{:T(128)} %constant.422.clone.1), kind=kCustom, calls=%fused_computation.34 | custom fusion | flops 3194880 | bytes 1672710 | tf_op jit(solution)/shard_map/scatter-add | solution.py:219
  239.0 14.9 %scatter_custom_fusion.2 = f32[257,384]{1,0:T(8,128)S(1)} fusion(s32[1664]{0:T(1024)S(1)} %fusion.151, bf16[640,384]{1,0:T(8,128)(2,1)} %collective-permute-done.5, bf16[]{:T(256)} %constant.487, bf16[1024,384]{1,0:T(8,128)(2,1)} %bitcast.41, f32[]{:T(128)} %constant.422.clone.1), kind=kCustom, calls=%fused_computation.36 | custom fusion | flops 3194880 | bytes 1672710 | tf_op jit(solution)/shard_map/scatter-add | solution.py:219
  262.3 2.7 collective-permute-start.9
  268.4 4.3 %collective-permute-done.10 = bf16[4,64,16]{2,1,0:T(8,128)(2,1)S(1)} collective-permute-done((bf16[4,64,16]{2,1,0:T(8,128)(2,1)S(1)}, bf16[4,64,16]{2,1,0:T(8,128)(2,1)S(1)}, u32[]{:S(2)}, u32[]{:S(2)}) %collective-permute-start.10) | collective-permute-done | bytes 8224 | tf_op jit(solution)/shard_map/ppermute | solution.py:34
  275.2 4.0 %gather_fusion.27 = f32[256,4,4,4]{3,2,1,0:T(4,128)S(1)} fusion(f32[4,4,4,288]{2,1,3,0:T(4,128)} %copy.2867, s32[1024]{0:T(1024)} %copy-done.72), kind=kCustom, calls=%fused_computation.24.clone | custom fusion | bytes 132096 | tf_op jit(solution)/shard_map/jit(_take)/gather | solution.py:97
  283.3 4.0 %gather_fusion.26 = f32[256,4,4,4]{3,2,1,0:T(4,128)S(1)} fusion(f32[4,4,4,288]{2,1,3,0:T(4,128)} %copy.2857, s32[1024]{0:T(1024)} %copy-done.71), kind=kCustom, calls=%fused_computation.23.clone | custom fusion | bytes 132096 | tf_op jit(solution)/shard_map/jit(_take)/gather | solution.py:97
  292.8 4.0 %gather_fusion.25 = f32[256,4,4,4]{3,2,1,0:T(4,128)S(1)} fusion(f32[4,4,4,288]{2,1,3,0:T(4,128)} %copy.2846, s32[1024]{0:T(1024)} %copy-done.70), kind=kCustom, calls=%fused_computation.22.clone | custom fusion | bytes 132096 | tf_op jit(solution)/shard_map/jit(_take)/gather | solution.py:97
  301.1 2.6 copy.2834
  303.8 4.0 %gather_fusion.24 = f32[256,4,4,4]{3,2,1,0:T(4,128)S(1)} fusion(f32[4,4,4,288]{2,1,3,0:T(4,128)} %copy.2834, s32[1024]{0:T(1024)} %copy-done.69), kind=kCustom, calls=%fused_computation.21.clone | custom fusion | bytes 132096 | tf_op jit(solution)/shard_map/jit(_take)/gather | solution.py:97
  315.1 4.0 %gather_fusion.23 = f32[256,4,4,4]{3,2,1,0:T(4,128)S(1)} fusion(f32[4,4,4,288]{2,1,3,0:T(4,128)} %bitcast.676, s32[1024]{0:T(1024)} %copy-done.68), kind=kCustom, calls=%fused_computation.20.clone | custom fusion | bytes 132096 | tf_op jit(solution)/shard_map/jit(_take)/gather | solution.py:97
  323.3 4.0 %gather_fusion.22 = f32[256,4,4,4]{3,2,1,0:T(4,128)S(1)} fusion(f32[4,4,4,288]{2,1,3,0:T(4,128)} %bitcast.677, s32[1024]{0:T(1024)} %copy-done.67), kind=kCustom, calls=%fused_computation.19.clone | custom fusion | bytes 132096 | tf_op jit(solution)/shard_map/jit(_take)/gather | solution.py:97
  (607 shorter events, 174.1 us)
Async XLA Ops:
  0.6 165.0 %copy-start = (f32[64,128]{1,0:T(8,128)S(1)}, f32[64,128]{1,0:T(8,128)}, u32[]{:S(2)}) copy-start(f32[64,128]{1,0:T(8,128)} %param.50) | copy-start | bytes 98308
  0.6 39.8 %copy-start.61 = (f32[3,64,64,1]{2,1,3,0:T(8,128)S(1)}, f32[3,64,64,1]{2,1,3,0:T(8,128)}, u32[]{:S(2)}) copy-start(f32[3,64,64,1]{2,1,3,0:T(8,128)} %constant.446) | copy-start | bytes 147460
  0.7 32.4 %copy-start.3 = (f32[1,4,64,256]{3,2,1,0:T(8,128)S(1)}, f32[1,4,64,256]{3,2,1,0:T(8,128)}, u32[]{:S(2)}) copy-start(f32[1,4,64,256]{3,2,1,0:T(8,128)} %param.51) | copy-start | bytes 786436
  0.7 32.5 %copy-start.64 = (s32[1,6,256]{2,0,1:T(1,128)S(1)}, s32[1,6,256]{2,0,1:T(1,128)}, u32[]{:S(2)}) copy-start(s32[1,6,256]{2,0,1:T(1,128)} %param.52) | copy-start | bytes 18436
  1.5 43.6 %collective-permute-start.2 = (s32[4,32]{1,0:T(4,128)S(1)}, s32[4,32]{1,0:T(4,128)S(1)}, u32[]{:S(2)}, u32[]{:S(2)}) collective-permute-start(s32[4,32]{1,0:T(4,128)S(1)} %get-tuple-element.340), channel_id=1, source_target_pairs={{0,1},{1,2},{2,3},{3,4},{4,5},{5,6},{6,7},{7,8},{8,9},{9,10},{10,1... | collective-permute-start | bytes 1544 | tf_op jit(solution)/shard_map/ppermute | solution.py:33
  5.5 41.5 %collective-permute-start.3 = (s32[4,32]{1,0:T(4,128)S(1)}, s32[4,32]{1,0:T(4,128)S(1)}, u32[]{:S(2)}, u32[]{:S(2)}) collective-permute-start(s32[4,32]{1,0:T(4,128)S(1)} %get-tuple-element.341), channel_id=1, source_target_pairs={{1,0},{2,1},{3,2},{4,3},{5,4},{6,5},{7,6},{8,7},{9,8},{10,9},{11,1... | collective-permute-start | bytes 1544 | tf_op jit(solution)/shard_map/ppermute | solution.py:34
  7.4 34.7 %copy-start.85 = (s32[1,6,256]{2,0,1:T(1,128)S(1)}, s32[1,6,256]{2,0,1:T(1,128)}, u32[]{:S(2)}) copy-start(s32[1,6,256]{2,0,1:T(1,128)} %param.53) | copy-start | bytes 18436
  9.2 104.8 %collective-permute-start = (f32[6,48,128]{2,1,0:T(8,128)}, f32[6,48,128]{2,1,0:T(8,128)}, u32[]{:S(2)}, u32[]{:S(2)}) collective-permute-start(f32[6,48,128]{2,1,0:T(8,128)} %get-tuple-element.273), channel_id=1, source_target_pairs={{0,1},{1,2},{2,3},{3,4},{4,5},{5,6},{6,7},{7,8},{8,9},{9,10},{10,1... | collective-permute-start | bytes 442376 | tf_op jit(solution)/shard_map/ppermute | solution.py:33
  14.9 99.1 %collective-permute-start.1 = (f32[6,48,128]{2,1,0:T(8,128)}, f32[6,48,128]{2,1,0:T(8,128)}, u32[]{:S(2)}, u32[]{:S(2)}) collective-permute-start(f32[6,48,128]{2,1,0:T(8,128)} %get-tuple-element.274), channel_id=1, source_target_pairs={{1,0},{2,1},{3,2},{4,3},{5,4},{6,5},{7,6},{8,7},{9,8},{10,9},{11,1... | collective-permute-start | bytes 442376 | tf_op jit(solution)/shard_map/ppermute | solution.py:34
  18.2 33.8 %all-to-all-start = ((s32[4,1,512]{2,1,0:T(1,128)}), s32[4,1,512]{2,1,0:T(1,128)S(1)}, u32[]{:S(2)}, u32[]{:S(2)}) async-start(s32[4,1,512]{2,1,0:T(1,128)} %broadcast_in_dim.469), calls=%async_computation | async-start | bytes 16384 | tf_op jit(solution)/shard_map/all_to_all | solution.py:41
  22.6 24.5 %copy-start.63 = (s32[1,4,256]{2,1,0:T(4,128)S(1)}, s32[1,4,256]{2,1,0:T(4,128)}, u32[]{:S(2)}) copy-start(s32[1,4,256]{2,1,0:T(4,128)} %param.48) | copy-start | bytes 12292
  23.6 42.0 %collective-permute-start.6 = (bf16[4,64,16]{2,1,0:T(8,128)(2,1)S(1)}, bf16[4,64,16]{2,1,0:T(8,128)(2,1)S(1)}, u32[]{:S(2)}, u32[]{:S(2)}) collective-permute-start(bf16[4,64,16]{2,1,0:T(8,128)(2,1)S(1)} %get-tuple-element.308), channel_id=1, source_target_pairs={{0,1},{1,2},{2,3},{3,4},{4,5},{5,6},{6,7},{7,8},{8,9},{9,10},{10,1... | collective-permute-start | bytes 24584 | tf_op jit(solution)/shard_map/ppermute | solution.py:33
  33.8 77.4 %copy-start.83 = (pred[256]{0:T(512)(128)(4,1)}, pred[256]{0:T(512)(128)(4,1)S(1)}, u32[]{:S(2)}) copy-start(pred[256]{0:T(512)(128)(4,1)S(1)} %get-tuple-element.374) | copy-start | bytes 772
  33.8 46.3 %copy-start.81 = (pred[256]{0:T(512)(128)(4,1)}, pred[256]{0:T(512)(128)(4,1)S(1)}, u32[]{:S(2)}) copy-start(pred[256]{0:T(512)(128)(4,1)S(1)} %get-tuple-element.373) | copy-start | bytes 772
  33.9 79.5 %copy-start.79 = (pred[256]{0:T(512)(128)(4,1)}, pred[256]{0:T(512)(128)(4,1)S(1)}, u32[]{:S(2)}) copy-start(pred[256]{0:T(512)(128)(4,1)S(1)} %get-tuple-element.372) | copy-start | bytes 772
  42.2 39.4 %copy-start.67 = (s32[1024]{0:T(1024)}, s32[1024]{0:T(1024)S(1)}, u32[]{:S(2)}) copy-start(s32[1024]{0:T(1024)S(1)} %pad_clamp_fusion.9) | copy-start | bytes 12292
  43.5 23.7 %copy-start.68 = (s32[1024]{0:T(1024)}, s32[1024]{0:T(1024)S(1)}, u32[]{:S(2)}) copy-start(s32[1024]{0:T(1024)S(1)} %pad_clamp_fusion.8) | copy-start | bytes 12292
  43.5 31.4 %copy-start.69 = (s32[1024]{0:T(1024)}, s32[1024]{0:T(1024)S(1)}, u32[]{:S(2)}) copy-start(s32[1024]{0:T(1024)S(1)} %pad_clamp_fusion.7) | copy-start | bytes 12292
  43.5 46.4 %copy-start.70 = (s32[1024]{0:T(1024)}, s32[1024]{0:T(1024)S(1)}, u32[]{:S(2)}) copy-start(s32[1024]{0:T(1024)S(1)} %pad_clamp_fusion.6) | copy-start | bytes 12292
  43.6 53.2 %copy-start.71 = (s32[1024]{0:T(1024)}, s32[1024]{0:T(1024)S(1)}, u32[]{:S(2)}) copy-start(s32[1024]{0:T(1024)S(1)} %pad_clamp_fusion.5) | copy-start | bytes 12292
  43.6 60.3 %copy-start.72 = (s32[1024]{0:T(1024)}, s32[1024]{0:T(1024)S(1)}, u32[]{:S(2)}) copy-start(s32[1024]{0:T(1024)S(1)} %pad_clamp_fusion.4) | copy-start | bytes 12292
  45.1 20.5 %collective-permute-start.7 = (bf16[4,64,16]{2,1,0:T(8,128)(2,1)S(1)}, bf16[4,64,16]{2,1,0:T(8,128)(2,1)S(1)}, u32[]{:S(2)}, u32[]{:S(2)}) collective-permute-start(bf16[4,64,16]{2,1,0:T(8,128)(2,1)S(1)} %get-tuple-element.309), channel_id=1, source_target_pairs={{1,0},{2,1},{3,2},{4,3},{5,4},{6,5},{7,6},{8,7},{9,8},{10,9},{11,1... | collective-permute-start | bytes 24584 | tf_op jit(solution)/shard_map/ppermute | solution.py:34
  53.8 18.7 %copy-start.134 = (s32[1024,1]{0,1:T(1,128)}, s32[1024,1]{0,1:T(1,128)S(1)}, u32[]{:S(2)}) copy-start(s32[1024,1]{0,1:T(1,128)S(1)} %compare_select_fusion.2) | copy-start | bytes 12292
  58.7 132.0 %collective-permute-start.4 = (s32[640]{0:T(1024)}, s32[640]{0:T(1024)}, u32[]{:S(2)}, u32[]{:S(2)}) collective-permute-start(s32[640]{0:T(1024)} %scatter_custom_fusion), channel_id=1, source_target_pairs={{0,1},{1,2},{2,3},{3,4},{4,5},{5,6},{6,7},{7,8},{8,9},{9,10},{10,1... | collective-permute-start | bytes 7688 | tf_op jit(solution)/shard_map/ppermute | solution.py:67
  133.5 29.2 %copy-start.1 = (f32[5,320,128]{2,1,0:T(8,128)}, f32[5,320,128]{2,1,0:T(8,128)S(1)}, u32[]{:S(2)}) copy-start(f32[5,320,128]{2,1,0:T(8,128)S(1)} %fusion.13) | copy-start | bytes 2457604
  167.8 14.9 %all-to-all-start.2 = ((bf16[4,1,256,384]{3,2,1,0:T(8,128)(2,1)}), bf16[4,1,256,384]{3,2,1,0:T(8,128)(2,1)S(1)}, u32[]{:S(2)}, u32[]{:S(2)}) async-start(bf16[4,1,256,384]{3,2,1,0:T(8,128)(2,1)} %broadcast_in_dim.513), calls=%async_computation.2 | async-start | bytes 1572864 | tf_op jit(solution)/shard_map/all_to_all | solution.py:41
  183.6 38.9 %copy-start.8 = (f32[1,5,256,128]{3,2,1,0:T(8,128)S(1)}, f32[1,5,256,128]{3,2,1,0:T(8,128)}, u32[]{:S(2)}) copy-start(f32[1,5,256,128]{3,2,1,0:T(8,128)} %param.45) | copy-start | bytes 1966084
  183.6 30.2 %all-to-all-start.1 = ((bf16[4,1,256,384]{3,2,1,0:T(8,128)(2,1)}), bf16[4,1,256,384]{3,2,1,0:T(8,128)(2,1)}, u32[]{:S(2)}, u32[]{:S(2)}) async-start(bf16[4,1,256,384]{3,2,1,0:T(8,128)(2,1)} %broadcast_in_dim.473), calls=%async_computation.1 | async-start | bytes 1572864 | tf_op jit(solution)/shard_map/all_to_all | solution.py:41
  210.8 12.6 %collective-permute-start.8 = (bf16[640,384]{1,0:T(8,128)(2,1)}, bf16[640,384]{1,0:T(8,128)(2,1)S(1)}, u32[]{:S(2)}, u32[]{:S(2)}) collective-permute-start(bf16[640,384]{1,0:T(8,128)(2,1)} %scatter_custom_fusion.4), channel_id=1, source_target_pairs={{0,1},{1,2},{2,3},{3,4},{4,5},{5,6},{6,7},{7,8},{8,9},{9,10},{10,1... | collective-permute-start | bytes 1474568 | tf_op jit(solution)/shard_map/ppermute | solution.py:67
  220.0 19.0 %collective-permute-start.5 = (bf16[640,384]{1,0:T(8,128)(2,1)}, bf16[640,384]{1,0:T(8,128)(2,1)}, u32[]{:S(2)}, u32[]{:S(2)}) collective-permute-start(bf16[640,384]{1,0:T(8,128)(2,1)} %scatter_custom_fusion.1), channel_id=1, source_target_pairs={{0,1},{1,2},{2,3},{3,4},{4,5},{5,6},{6,7},{7,8},{8,9},{9,10},{10,1... | collective-permute-start | bytes 1474568 | tf_op jit(solution)/shard_map/ppermute | solution.py:67
  262.3 6.1 %collective-permute-start.9 = (bf16[4,64,16]{2,1,0:T(8,128)(2,1)S(1)}, bf16[4,64,16]{2,1,0:T(8,128)(2,1)S(1)}, u32[]{:S(2)}, u32[]{:S(2)}) collective-permute-start(bf16[4,64,16]{2,1,0:T(8,128)(2,1)S(1)} %get-tuple-element.306), channel_id=1, source_target_pairs={{0,1},{1,2},{2,3},{3,4},{4,5},{5,6},{6,7},{7,8},{8,9},{9,10},{10,1... | collective-permute-start | bytes 24584 | tf_op jit(solution)/shard_map/ppermute | solution.py:33
  265.0 7.7 %collective-permute-start.10 = (bf16[4,64,16]{2,1,0:T(8,128)(2,1)S(1)}, bf16[4,64,16]{2,1,0:T(8,128)(2,1)S(1)}, u32[]{:S(2)}, u32[]{:S(2)}) collective-permute-start(bf16[4,64,16]{2,1,0:T(8,128)(2,1)S(1)} %get-tuple-element.307), channel_id=1, source_target_pairs={{1,0},{2,1},{3,2},{4,3},{5,4},{6,5},{7,6},{8,7},{9,8},{10,9},{11,1... | collective-permute-start | bytes 24584 | tf_op jit(solution)/shard_map/ppermute | solution.py:34
  (130 other events, 772.4 us)
where the time goes:
time: 347 us; the launch traced here: 341 us
  local copies, waits for them, and re-layouts  181 us (52%)
  other arithmetic  97.1 us (28%)
  starting transfers between devices  50.1 us (14%)
  matrix products  4.45 us (1%)
  waiting for transfers between devices  4.36 us (1%)
  between operations  4.19 us (1%)
    gather x40, local copies, waits for them, and re-layouts, near_take(): return jnp.take(field, links, axis=dimension)  94.5 us
    scatter-add x2, other arithmetic, gather_sources(): jnp.zeros((count + 1, rows.shape[1]), jnp.float32).at[index]  30.4 us
    ppermute x4, starting transfers between devices, with_halo(): before = lax.ppermute(last, axis, up)  18.8 us
    all_to_all x3, starting transfers between devices, copy_for_each(): lax.all_to_all(jnp.broadcast_to(x[None], (count, *x.shape)), axis, 0, 0,...  13 us
    scatter-add x1, other arithmetic, gather_sources(): counts = jnp.zeros((count + 1,), jnp.float32).at[index].add(jnp.where(ids...  12.7 us
    scatter x2, local copies, waits for them, and re-layouts, body(): passed = jnp.zeros((groups * CAP, width), jnp.bfloat16).at[slot].set(got_...  12.2 us
    ppermute x3, starting transfers between devices, shifted(): lax.ppermute(value, axis, [(source, source + steps) for source in range(f...  10.7 us
    sub x2, other arithmetic, flow_advance(): return center + viscosity * laplace - ADVECT * advection  8.8 us
  transfers between devices with their start and end apart: 14, of which 1 were waited for; matrix products, arithmetic and copies ran while one was open for 56% of the time, Pallas kernels for 0%

commit v1 on v0

v1 whole, which is shorter than its diff:
```python
import functools

import jax
import jax.numpy as jnp
import numpy as np
from jax import lax
from jax.experimental import pallas as pl
from jax.experimental.pallas import tpu as pltpu
from jax.sharding import PartitionSpec as P

MESH = pl.DeviceIdType.MESH
F32 = jnp.float32
BF16 = jnp.bfloat16

HW = 16
FT = 256
CELLS = 128
HALO = 3 * HW
WIDE = FT + 2 * HALO
BAND = 160
EL = 256
NP = 64
TURNS = 2


def derivative_operators():
    points = np.array([-1.0, -1.0 / np.sqrt(5.0), 1.0 / np.sqrt(5.0), 1.0])
    weights = np.array(
        [
            1.0 / np.prod([points[col] - points[other] for other in range(4) if other != col])
            for col in range(4)
        ]
    )
    matrix = np.zeros((4, 4))
    for line in range(4):
        for col in range(4):
            if line != col:
                matrix[line, col] = weights[col] / weights[line] / (points[line] - points[col])
        matrix[line, line] = -matrix[line].sum()
    eye = np.eye(4)
    return np.concatenate(
        [
            np.kron(eye, np.kron(eye, matrix)),
            np.kron(eye, np.kron(matrix, eye)),
            np.kron(matrix, np.kron(eye, eye)),
        ]
    ).astype(np.float32)


def face_tables():
    faces = []
    for face in range(6):
        axis, level = face // 2, 3 * (face % 2)
        members = []
        for second in range(4):
            for first in range(4):
                coords = [first, second]
                coords.insert(axis, level)
                members.append(coords[0] + 4 * coords[1] + 16 * coords[2])
        faces.append(members)
    turns = []
    for turn in range(4):
        mapping = []
        for second in range(4):
            for first in range(4):
                source = ((first, second), (3 - second, first), (3 - first, 3 - second), (second, 3 - first))[turn]
                mapping.append(source[0] + 4 * source[1])
        turns.append(mapping)
    return faces, turns


def constants():
    deriv = jnp.asarray(derivative_operators())
    high = deriv.astype(BF16)
    low = (deriv - high.astype(F32)).astype(BF16)
    deriv3 = jnp.concatenate([high, high, low], 1)
    faces, turns = face_tables()
    pick = np.zeros((96, NP), np.float32)
    put = np.zeros((NP, 4 * 96), np.float32)
    for face in range(6):
        for p in range(16):
            pick[16 * face + p, faces[face ^ 1][p]] = 1
            for turn in range(4):
                put[faces[face][p], 96 * turn + 16 * face + turns[turn][p]] = 1
    return deriv3, jnp.asarray(pick, BF16), jnp.asarray(put, BF16)


def halves(x):
    high = x.astype(BF16)
    return high, (x - high.astype(F32)).astype(BF16)


def dot(a, b):
    return lax.dot_general(a, b, (((1,), (0,)), ((), ())), preferred_element_type=F32)


def dot_t(a, b):
    return lax.dot_general(a, b, (((1,), (1,)), ((), ())), preferred_element_type=F32)


def kernel(
    n_sfc,
    ff, mv, cv, tl, tt, pj, ac, en, fc, d3_h, pick_h, put_h,
    fo, mo, ao,
    w0, w1, vis, lk, mean, sel, xb, pay, tgt, oht, pb, res, proj,
    st, sb, hl, hr, enb, fcb, d3, pick, put, ohf, grad, src,
    ls, hs, hrs, ts, trs, ps, prs, rs, rrs, as_, ars, outs,
):
    g = lax.axis_index("grp")
    s = lax.axis_index("sfc")
    right = lax.rem(s + 1, n_sfc)
    left = lax.rem(s + n_sfc - 1, n_sfc)
    first = s * FT
    barrier = pltpu.get_barrier_semaphore()

    def greet(gg, ss):
        pl.semaphore_signal(barrier, inc=1, device_id=(gg, ss), device_id_type=MESH)

    @pl.when(g < 3)
    def _():
        greet(3, s)
        for d in range(3):
            w = lax.rem(g + d, 3)
            if d:
                greet(w, s)
            greet(w, right)
            greet(w, left)

    @pl.when(g == 3)
    def _():
        for w in range(3):
            greet(w, s)
        greet(3, left)
        greet(3, right)

    def load(source, target, k):
        copy = pltpu.make_async_copy(source, target, ls.at[k])
        copy.start()
        return copy

    def remote(source, target, send, recv, gg, ss):
        return pltpu.make_async_remote_copy(
            src_ref=source, dst_ref=target, send_sem=send, recv_sem=recv,
            device_id=(gg, ss), device_id_type=MESH,
        )

    load_state = load(ff, w0.at[:, HALO : HALO + FT, :], 0)
    load_mean = load(mv, mean, 1)
    load_sound = load(ac, st, 2)

    @pl.when(g < 3)
    def _():
        loads = [
            load(cv, vis.at[HALO : HALO + FT, :], 3),
            load(tl, lk.at[0:4, 128 : 128 + FT], 4),
            load(tt, tgt.at[0], 5),
            load(pj, proj, 6),
        ]
        pl.semaphore_wait(barrier, 9)
        halo = []
        for k, (source, target) in enumerate(
            (
                (ff.at[:, 0:HALO, :], w0.at[:, HALO + FT : WIDE, :]),
                (cv.at[0:HALO, :], vis.at[HALO + FT : WIDE, :]),
                (tl.at[:, 0:128], lk.at[0:4, 128 + FT : 256 + FT]),
            )
        ):
            halo.append(remote(source, target, hs.at[k], hrs.at[k], g, left))
        for k, (source, target) in enumerate(
            (
                (ff.at[:, FT - HALO : FT, :], w0.at[:, 0:HALO, :]),
                (cv.at[FT - HALO : FT, :], vis.at[0:HALO, :]),
                (tl.at[:, FT - 128 : FT], lk.at[0:4, 0:128]),
            )
        ):
            halo.append(remote(source, target, hs.at[3 + k], hrs.at[3 + k], g, right))
        for k in (0, 3, 2, 5, 1, 4):
            halo[k].start()
        targets = []
        for d in range(3):
            w = lax.rem(g + d, 3)
            for h, ss in ((0, s), (1, right)):
                if d or h:
                    k = 2 * d + h
                    copy = remote(tt, tgt.at[k], ts.at[k], trs.at[k], w, ss)
                    copy.start()
                    targets.append(copy)
        lk[4:8, :] = jnp.zeros((4, 2 * 128 + FT), jnp.int32)
        for copy in loads:
            copy.wait()
        load_state.wait()
        load_mean.wait()
        for copy in halo:
            copy.wait()

        cols = lax.broadcasted_iota(jnp.int32, (BAND, 256), 1)
        own = lax.broadcasted_iota(jnp.int32, (BAND, 1), 0)
        lt = jnp.transpose(lk[...])
        for b in range(2):
            links = lt[96 + BAND * b : 96 + BAND * (b + 1), :]
            hot = []
            for k in range(4):
                link = links[:, k : k + 1]
                at = jnp.where(
                    link < 0, own + (HW + BAND * b - 96 * b), link - (first - HALO + 96 * b)
                )
                hot.append(jnp.where(cols == at, F32(1.0), F32(0.0)))
            sel[b, 0:BAND, :] = (hot[0] + hot[1] + hot[2] + hot[3]).astype(BF16)
            sel[b, BAND : 2 * BAND, :] = (hot[0] - hot[1]).astype(BF16)
            sel[b, 2 * BAND : 3 * BAND, :] = (hot[2] - hot[3]).astype(BF16)

        ph, plow = halves(proj[...])
        p2 = jnp.concatenate([ph, ph], 1)

        def gather(b, window):
            r = dot(sel[b], jnp.concatenate(halves(window), 1))
            r = r[:, :CELLS] + r[:, CELLS:]
            return r[0:BAND], r[BAND : 2 * BAND], r[2 * BAND :]

        def east_west(c):
            return pltpu.roll(c, CELLS - 1, 1), pltpu.roll(c, 1, 1)

        def advance(source, target, b, fields):
            r0, c0 = HW + BAND * b, 96 * b
            velocity = [source[f, r0 : r0 + BAND, :] for f in (1, 2, 3)]
            nu = vis[r0 : r0 + BAND, :]
            differences = []
            for f in fields:
                c = source[f, r0 : r0 + BAND, :]
                around, d2, d3_ = gather(b, source[f, c0 : c0 + 256, :])
                east, west = east_west(c)
                d1 = east - west
                target[f, r0 : r0 + BAND, :] = (
                    c
                    + nu * (east + west + around - 6.0 * c)
                    - 0.05 * (velocity[0] * d1 + velocity[1] * d2 + velocity[2] * d3_)
                )
                differences.append((d1, d2, d3_))
            return velocity, differences

        def sources(b, velocity, differences, turn):
            (u1, u2, u3), (v1, v2, v3), (w1_, w2_, w3_) = differences
            u, v, w = velocity
            vx = 0.5 * (w2_ - v3)
            vy = 0.5 * (u3 - w1_)
            vz = 0.5 * (v1 - u2)
            packed = [vy * w - vz * v, vz * u - vx * w, vx * v - vy * u]
            rows = slice(128 * b, 128 * b + 128)
            for k in range(3):
                m = 0.9 * mean[k, rows, :] + 0.1 * velocity[k]
                mean[k, rows, :] = m
                packed.append(m)
            for k in range(6):
                hi, lo = halves(packed[k])
                xb[k, rows, 0:128] = hi
                xb[k, rows, 128:256] = lo

        def own_rows(b, x):
            o = 2 * HW if b == 0 else 0
            return x[o : o + 128]

        def send_payload(turn):
            for k in range(6):
                x = xb[k]
                pay[turn, NP * k : NP * (k + 1), :] = (
                    dot_t(p2, x) + dot_t(plow, x[:, 0:128])
                ).astype(BF16)
            copies = []
            for d in (1, 2, 0):
                w = lax.rem(g + d, 3)
                for h, ss in ((0, s), (1, right)):
                    if d or h:
                        k = 2 * d + h
                        copy = remote(
                            pay.at[turn, pl.ds(pl.multiple_of(128 * w, 128), 128), :],
                            pb.at[turn, k], ps.at[turn, k], prs.at[turn, k], w, ss,
                        )
                        copy.start()
                        copies.append(copy)
            return copies

        for b in range(2):
            advance(w0, w1, b, (0, 1, 2, 3, 4))
        w1[:, 0:HW, :] = w0[:, 0:HW, :]
        w1[:, WIDE - HW : WIDE, :] = w0[:, WIDE - HW : WIDE, :]
        for b in range(2):
            velocity, differences = advance(w1, w0, b, (1, 2, 3))
            sources(
                b,
                [own_rows(b, x) for x in velocity],
                [[own_rows(b, x) for x in d] for d in differences],
                0,
            )
        payloads = [send_payload(0)]
        for b in range(2):
            o = HALO + 128 * b
            c0 = 96 * b
            velocity, differences = [], []
            i0 = 2 * HW if b == 0 else 0
            rows = jnp.concatenate(
                [
                    sel[b, BAND + i0 : BAND + i0 + 128, :],
                    sel[b, 2 * BAND + i0 : 2 * BAND + i0 + 128, :],
                ],
                0,
            )
            for f in (1, 2, 3):
                c = w0[f, o : o + 128, :]
                r = dot(rows, jnp.concatenate(halves(w0[f, c0 : c0 + 256, :]), 1))
                r = r[:, :CELLS] + r[:, CELLS:]
                east, west = east_west(c)
                velocity.append(c)
                differences.append((east - west, r[0:128], r[128:256]))
            sources(b, velocity, differences, 1)
        payloads.append(send_payload(1))
        for b in range(2):
            advance(w1, w0, b, (0, 4))

        for copy in targets:
            copy.wait()
        element = lax.broadcasted_iota(jnp.int32, (EL, FT), 0) + s * EL
        count = jnp.zeros((16, EL), F32)
        ones = jnp.ones((16, FT), BF16)
        for k in range(6):
            hot = jnp.where(tgt[k] == element, F32(1.0), F32(0.0)).astype(BF16)
            oht[k] = hot
            count = count + dot_t(ones, hot)
        inverse = 1.0 / jnp.maximum(count[0:1], 1.0)
        results = []
        mine = pl.ds(pl.multiple_of(128 * g, 128), 128)
        for turn in range(TURNS):
            total = dot_t(pay[turn, mine, :], oht[0])
            for copy in payloads[turn]:
                copy.wait()
            for k in range(1, 6):
                total = total + dot_t(pb[turn, k], oht[k])
            res[turn] = (total * inverse).astype(BF16)
            copy = remote(res.at[turn], src.at[turn, mine, :], rs.at[turn], rrs.at[turn, g], 3, s)
            copy.start()
            results.append(copy)
        load_sound.wait()
        writes = [
            pltpu.make_async_copy(w0.at[:, HALO : HALO + FT, :], fo, outs.at[0]),
            pltpu.make_async_copy(mean, mo, outs.at[1]),
            pltpu.make_async_copy(st, ao, outs.at[2]),
        ]
        for copy in writes:
            copy.start()
        for copy in results:
            copy.wait_send()
        for copy in writes:
            copy.wait()

    @pl.when(g == 3)
    def _():
        loads = [
            load(en, enb, 3),
            load(fc, fcb, 4),
            load(d3_h, d3, 5),
            load(pick_h, pick, 6),
            load(put_h, put, 7),
        ]
        pl.semaphore_wait(barrier, 5)
        load_sound.wait()

        def send_state(turn):
            for v in range(4):
                sb[turn, NP * v : NP * (v + 1), :] = st[v].astype(BF16)
            copies = [
                remote(sb.at[turn, :, 0:128], hr.at[turn], as_.at[turn, 0], ars.at[turn, 0], 3, left),
                remote(sb.at[turn, :, 128:256], hl.at[turn], as_.at[turn, 1], ars.at[turn, 1], 3, right),
            ]
            for copy in copies:
                copy.start()
            return copies

        sends = send_state(0)
        load_state.wait()
        load_mean.wait()
        writes = [
            pltpu.make_async_copy(w0.at[:, HALO : HALO + FT, :], fo, outs.at[0]),
            pltpu.make_async_copy(mean, mo, outs.at[1]),
        ]
        for copy in writes:
            copy.start()
        for copy in loads:
            copy.wait()

        row = lax.broadcasted_iota(jnp.int32, (EL + 128, EL), 0)
        for f in range(6):
            link = enb[f : f + 1, :]
            at = link - s * EL
            at = jnp.where(link < 0, 999, jnp.where(at < 0, at + (EL + 128), at))
            ohf[f] = jnp.where(row == at, F32(1.0), F32(0.0)).astype(BF16)
        node = lax.broadcasted_iota(jnp.int32, (NP, EL), 0)
        faces_on = jnp.zeros((NP, EL), F32)
        for f in range(6):
            coordinate = (node >> (2 * (f // 2))) & 3
            valid = jnp.where(enb[f : f + 1, :] >= 0, F32(1.0), F32(0.0))
            faces_on = faces_on + jnp.where(coordinate == 3 * (f % 2), valid, F32(0.0))
        lane = lax.broadcasted_iota(jnp.int32, (4 * NP, 128), 1)

        for turn in range(TURNS):
            for v in range(4):
                hi, lo = halves(st[v])
                grad[v] = dot(d3[...], jnp.concatenate([hi, lo, hi], 0))
            for copy in sends:
                copy.wait()
            ends = jnp.where(lane < HW, hr[turn].astype(F32), hl[turn].astype(F32)).astype(BF16)
            facing = []
            for v in range(4):
                rows = slice(NP * v, NP * (v + 1))
                wide = jnp.concatenate([sb[turn, rows, :], ends[rows]], 1)
                facing.append(dot(pick[...], wide).astype(BF16))
            remotes = []
            for f in range(6):
                stacked = jnp.concatenate([facing[v][16 * f : 16 * f + 16] for v in range(4)], 0)
                remotes.append(dot(stacked, ohf[f]))
            before = []
            for v in range(4):
                turned = []
                for r in range(4):
                    for f in range(6):
                        turned.append(
                            jnp.where(
                                fcb[f : f + 1, :] == r, remotes[f][16 * v : 16 * v + 16], F32(0.0)
                            ).astype(BF16)
                        )
                jump = dot(put[...], jnp.concatenate(turned, 0)) - faces_on * st[v]
                if v == 0:
                    linear = grad[1, 0:64] + grad[2, 64:128] + grad[3, 128:192]
                else:
                    linear = grad[0, 64 * (v - 1) : 64 * v]
                before.append(st[v] + 0.08 * (1.5 * jump - linear))
            for w in range(3):
                rows = slice(128 * w, 128 * w + 128)
                remote(
                    res.at[turn], src.at[turn, rows, :], rs.at[turn], rrs.at[turn, w], w, s
                ).wait_recv()
            flow = [src[turn, 192 + 64 * d : 256 + 64 * d, :].astype(F32) for d in range(3)]
            for v in range(4):
                convect = sum(flow[d] * grad[v, 64 * d : 64 * d + 64] for d in range(3))
                if v:
                    convect = convect + src[turn, 64 * (v - 1) : 64 * v, :].astype(F32)
                st[v] = before[v] - 0.08 * convect
            if turn == 0:
                sends = send_state(1)
        write = pltpu.make_async_copy(st, ao, outs.at[2])
        write.start()
        for copy in writes:
            copy.wait()
        write.wait()


def body(ff, mv, cv, tl, tt, pj, ac, en, fc):
    n_sfc = lax.axis_size("sfc")
    any_space = pl.BlockSpec(memory_space=pl.ANY)
    dma = pltpu.SemaphoreType.DMA
    outs = pl.pallas_call(
        functools.partial(kernel, n_sfc),
        out_shape=(
            jax.ShapeDtypeStruct((5, FT, CELLS), F32),
            jax.ShapeDtypeStruct((3, FT, CELLS), F32),
            jax.ShapeDtypeStruct((4, NP, EL), F32),
        ),
        in_specs=[any_space] * 12,
        out_specs=(any_space,) * 3,
        scratch_shapes=[
            pltpu.VMEM((5, WIDE, CELLS), F32),
            pltpu.VMEM((5, WIDE, CELLS), F32),
            pltpu.VMEM((WIDE, CELLS), F32),
            pltpu.VMEM((8, 256 + FT), jnp.int32),
            pltpu.VMEM((3, FT, CELLS), F32),
            pltpu.VMEM((2, 3 * BAND, 256), BF16),
            pltpu.VMEM((6, FT, 256), BF16),
            pltpu.VMEM((TURNS, 6 * NP, FT), BF16),
            pltpu.VMEM((6, 1, FT), jnp.int32),
            pltpu.VMEM((6, EL, FT), BF16),
            pltpu.VMEM((TURNS, 6, 128, FT), BF16),
            pltpu.VMEM((TURNS, 128, EL), BF16),
            pltpu.VMEM((NP, CELLS), F32),
            pltpu.VMEM((4, NP, EL), F32),
            pltpu.VMEM((TURNS, 4 * NP, EL), BF16),
            pltpu.VMEM((TURNS, 4 * NP, 128), BF16),
            pltpu.VMEM((TURNS, 4 * NP, 128), BF16),
            pltpu.VMEM((6, EL), jnp.int32),
            pltpu.VMEM((6, EL), jnp.int32),
            pltpu.VMEM((192, 192), BF16),
            pltpu.VMEM((96, NP), BF16),
            pltpu.VMEM((NP, 384), BF16),
            pltpu.VMEM((6, EL + 128, EL), BF16),
            pltpu.VMEM((4, 192, EL), F32),
            pltpu.VMEM((TURNS, 6 * NP, EL), BF16),
            dma((8,)),
            dma((6,)), dma((6,)),
            dma((6,)), dma((6,)),
            dma((TURNS, 6)), dma((TURNS, 6)),
            dma((TURNS,)), dma((TURNS, 3)),
            dma((TURNS, 2)), dma((TURNS, 2)),
            dma((3,)),
        ],
        compiler_params=pltpu.CompilerParams(
            collective_id=0, has_side_effects=True, vmem_limit_bytes=48 * 1024 * 1024
        ),
    )(ff[0], mv[0], cv[0], tl[0], tt, pj, ac[0], en[0], fc[0], *constants())
    return tuple(o[None] for o in outs)


def solution(mesh):
    placed = (
        P("grp", None, "sfc", None),
        P("grp", None, "sfc", None),
        P("grp", "sfc", None),
        P("grp", None, "sfc"),
        P("grp", "sfc"),
        P(),
        P("grp", None, None, "sfc"),
        P("grp", None, "sfc"),
        P("grp", None, "sfc"),
    )
    return jax.shard_map(
        body,
        mesh=mesh,
        in_specs=placed,
        out_specs=(
            P("grp", None, "sfc", None),
            P("grp", None, "sfc", None),
            P("grp", None, None, "sfc"),
        ),
        check_vma=False,
    )
```

time: 347 us -> 42.1 us (0.12)
  the two profiles are of different devices: /device:TPU:47 before, /device:TPU:24 now
where the time goes in v1:
time: 42.1 us; the launch traced here: 41.6 us
  Pallas kernels  30.9 us (73%)
  local copies, waits for them, and re-layouts  10.1 us (24%)
  between operations  0.67 us (2%)
    pallas_call x1, Pallas kernels, body(): pl.pallas_call(functools.partial(kernel, n_sfc), out_shape=(jax.ShapeDtyp...  30.9 us
    unnamed x24, local copies, waits for them, and re-layouts  10.1 us

profile of v1, /device:TPU:24, one launch (start us, length us, event | category | flops | bytes accessed | tf_op | source)
XLA Modules:
  0.0 41.6 jit_solution(9945960580885537768)
XLA Ops:
  0.6 0.0 copy-start.6
  0.6 0.0 copy-start.8
  0.7 0.7 %copy_bitcast_fusion = (s32[6,256]{1,0:T(8,128)S(1)}, s32[6,256]{1,0:T(8,128)S(1)}) fusion(s32[1,6,256]{2,0,1:T(1,128)} %param.20, s32[1,6,256]{2,0,1:T(1,128)} %param.19), kind=kLoop, calls=%fused_computation | loop fusion | bytes 24576
  1.4 0.0 copy-start.9
  1.4 0.0 copy-done.6
  1.4 0.0 copy-done.8
  1.4 0.7 %copy-done.9 = s32[1,256]{1,0:T(1,128)S(1)} copy-done((s32[1,256]{1,0:T(1,128)S(1)}, s32[1,256]{1,0:T(1,128)}, u32[]{:S(2)}) %copy-start.9) | copy-done | bytes 1048
  2.1 0.0 copy-start
  2.1 1.1 %copy-done = f32[1,5,256,128]{3,2,1,0:T(8,128)S(1)} copy-done((f32[1,5,256,128]{3,2,1,0:T(8,128)S(1)}, f32[1,5,256,128]{3,2,1,0:T(8,128)}, u32[]{:S(2)}) %copy-start) | copy-done | bytes 655384
  3.1 0.0 copy-start.1
  3.1 1.0 %copy-done.1 = f32[1,3,256,128]{3,2,1,0:T(8,128)S(1)} copy-done((f32[1,3,256,128]{3,2,1,0:T(8,128)S(1)}, f32[1,3,256,128]{3,2,1,0:T(8,128)}, u32[]{:S(2)}) %copy-start.1) | copy-done | bytes 393240
  4.1 0.0 copy-start.2
  4.1 0.9 %copy-done.2 = f32[1,4,64,256]{3,2,1,0:T(8,128)S(1)} copy-done((f32[1,4,64,256]{3,2,1,0:T(8,128)S(1)}, f32[1,4,64,256]{3,2,1,0:T(8,128)}, u32[]{:S(2)}) %copy-start.2) | copy-done | bytes 262168
  5.1 0.0 copy-start.3
  5.1 0.9 %copy-done.3 = f32[1,256,128]{2,1,0:T(8,128)S(1)} copy-done((f32[1,256,128]{2,1,0:T(8,128)S(1)}, f32[1,256,128]{2,1,0:T(8,128)}, u32[]{:S(2)}) %copy-start.3) | copy-done | bytes 131096
  6.0 0.0 copy-start.4
  6.0 0.9 %copy-done.4 = bf16[192,192]{1,0:T(8,128)(2,1)S(1)} copy-done((bf16[192,192]{1,0:T(8,128)(2,1)S(1)}, bf16[192,192]{1,0:T(8,128)(2,1)}, u32[]{:S(2)}) %copy-start.4) | copy-done | bytes 73752
  6.9 0.0 copy-start.5
  6.9 0.8 %copy-done.5 = bf16[64,384]{1,0:T(8,128)(2,1)S(1)} copy-done((bf16[64,384]{1,0:T(8,128)(2,1)S(1)}, bf16[64,384]{1,0:T(8,128)(2,1)}, u32[]{:S(2)}) %copy-start.5) | copy-done | bytes 49176
  7.7 0.0 copy-start.7
  7.7 0.7 %copy-done.7 = bf16[96,64]{1,0:T(8,128)(2,1)S(1)} copy-done((bf16[96,64]{1,0:T(8,128)(2,1)S(1)}, bf16[96,64]{1,0:T(8,128)(2,1)}, u32[]{:S(2)}) %copy-start.7) | copy-done | bytes 12312
  8.4 30.9 %shard_map.139 = (f32[5,256,128]{2,1,0:T(8,128)S(1)}, f32[3,256,128]{2,1,0:T(8,128)S(1)}, f32[4,64,256]{2,1,0:T(8,128)S(1)}) custom-call(f32[5,256,128]{2,1,0:T(8,128)S(1)} %bitcast.12, f32[3,256,128]{2,1,0:T(8,128)S(1)} %bitcast.15, f32[256,128]{1,0:T(8,128)S(1)} %bitcast.18, s32[4,256]{1,0:T(4,128)S(1)} %bitcast.19, s32[1,256]{1,0:T(1,128)S(1)} %copy-done.9, ...), custom_call_target="tpu_custom_call" | custom-call | tf_op jit(solution)/shard_map/pallas_call | solution.py:459
  39.3 0.8 %copy.22 = f32[1,5,256,128]{3,2,1,0:T(8,128)} copy(f32[1,5,256,128]{3,2,1,0:T(8,128)S(1)} %bitcast.13) | data formatting | bytes 1310720
  40.1 0.7 %copy.23 = f32[1,3,256,128]{3,2,1,0:T(8,128)} copy(f32[1,3,256,128]{3,2,1,0:T(8,128)S(1)} %bitcast.14) | data formatting | bytes 786432
  40.9 0.7 %copy.24 = f32[1,4,64,256]{3,2,1,0:T(8,128)} copy(f32[1,4,64,256]{3,2,1,0:T(8,128)S(1)} %bitcast.16) | data formatting | bytes 524288
Async XLA Ops:
  0.6 0.8 %copy-start.6 = (f32[64,128]{1,0:T(8,128)S(1)}, f32[64,128]{1,0:T(8,128)}, u32[]{:S(2)}) copy-start(f32[64,128]{1,0:T(8,128)} %pj.1) | copy-start | bytes 98308
  0.6 0.8 %copy-start.8 = (s32[1,4,256]{2,1,0:T(4,128)S(1)}, s32[1,4,256]{2,1,0:T(4,128)}, u32[]{:S(2)}) copy-start(s32[1,4,256]{2,1,0:T(4,128)} %param.15) | copy-start | bytes 12292
  1.4 0.7 %copy-start.9 = (s32[1,256]{1,0:T(1,128)S(1)}, s32[1,256]{1,0:T(1,128)}, u32[]{:S(2)}) copy-start(s32[1,256]{1,0:T(1,128)} %tt.1) | copy-start | bytes 3076
  2.1 1.1 %copy-start = (f32[1,5,256,128]{3,2,1,0:T(8,128)S(1)}, f32[1,5,256,128]{3,2,1,0:T(8,128)}, u32[]{:S(2)}) copy-start(f32[1,5,256,128]{3,2,1,0:T(8,128)} %param.12) | copy-start | bytes 1966084
  3.1 1.0 %copy-start.1 = (f32[1,3,256,128]{3,2,1,0:T(8,128)S(1)}, f32[1,3,256,128]{3,2,1,0:T(8,128)}, u32[]{:S(2)}) copy-start(f32[1,3,256,128]{3,2,1,0:T(8,128)} %param.13) | copy-start | bytes 1179652
  4.1 0.9 %copy-start.2 = (f32[1,4,64,256]{3,2,1,0:T(8,128)S(1)}, f32[1,4,64,256]{3,2,1,0:T(8,128)}, u32[]{:S(2)}) copy-start(f32[1,4,64,256]{3,2,1,0:T(8,128)} %param.18) | copy-start | bytes 786436
  5.1 0.9 %copy-start.3 = (f32[1,256,128]{2,1,0:T(8,128)S(1)}, f32[1,256,128]{2,1,0:T(8,128)}, u32[]{:S(2)}) copy-start(f32[1,256,128]{2,1,0:T(8,128)} %param.14) | copy-start | bytes 393220
  6.0 0.9 %copy-start.4 = (bf16[192,192]{1,0:T(8,128)(2,1)S(1)}, bf16[192,192]{1,0:T(8,128)(2,1)}, u32[]{:S(2)}) copy-start(bf16[192,192]{1,0:T(8,128)(2,1)} %constant.21.d3_h) | copy-start | bytes 221188
  6.9 0.8 %copy-start.5 = (bf16[64,384]{1,0:T(8,128)(2,1)S(1)}, bf16[64,384]{1,0:T(8,128)(2,1)}, u32[]{:S(2)}) copy-start(bf16[64,384]{1,0:T(8,128)(2,1)} %constant.8.clone.put_h) | copy-start | bytes 147460
  7.7 0.7 %copy-start.7 = (bf16[96,64]{1,0:T(8,128)(2,1)S(1)}, bf16[96,64]{1,0:T(8,128)(2,1)}, u32[]{:S(2)}) copy-start(bf16[96,64]{1,0:T(8,128)(2,1)} %constant.7.clone.pick_h) | copy-start | bytes 36868

commit v2 on v1

--- a/solution.py
+++ b/solution.py
@@ -388,7 +388,7 @@
 
         row = lax.broadcasted_iota(jnp.int32, (EL + 128, EL), 0)
         for f in range(6):
-            link = enb[f : f + 1, :]
+            link = enb[f]
             at = link - s * EL
             at = jnp.where(link < 0, 999, jnp.where(at < 0, at + (EL + 128), at))
             ohf[f] = jnp.where(row == at, F32(1.0), F32(0.0)).astype(BF16)
@@ -396,7 +396,7 @@
         faces_on = jnp.zeros((NP, EL), F32)
         for f in range(6):
             coordinate = (node >> (2 * (f // 2))) & 3
-            valid = jnp.where(enb[f : f + 1, :] >= 0, F32(1.0), F32(0.0))
+            valid = jnp.where(enb[f] >= 0, F32(1.0), F32(0.0))
             faces_on = faces_on + jnp.where(coordinate == 3 * (f % 2), valid, F32(0.0))
         lane = lax.broadcasted_iota(jnp.int32, (4 * NP, 128), 1)
 
@@ -423,7 +423,7 @@
                     for f in range(6):
                         turned.append(
                             jnp.where(
-                                fcb[f : f + 1, :] == r, remotes[f][16 * v : 16 * v + 16], F32(0.0)
+                                fcb[f] == r, remotes[f][16 * v : 16 * v + 16], F32(0.0)
                             ).astype(BF16)
                         )
                 jump = dot(put[...], jnp.concatenate(turned, 0)) - faces_on * st[v]
@@ -452,8 +452,20 @@
         write.wait()
 
 
+def store(a, b, c, x, y, z, sems):
+    copies = [
+        pltpu.make_async_copy(source, target, sems.at[k])
+        for k, (source, target) in enumerate(((a, x), (b, y), (c, z)))
+    ]
+    for copy in copies:
+        copy.start()
+    for copy in copies:
+        copy.wait()
+
+
 def body(ff, mv, cv, tl, tt, pj, ac, en, fc):
     n_sfc = lax.axis_size("sfc")
+    hbm = pl.BlockSpec(memory_space=pltpu.MemorySpace.HBM)
     any_space = pl.BlockSpec(memory_space=pl.ANY)
     dma = pltpu.SemaphoreType.DMA
     outs = pl.pallas_call(
@@ -463,7 +475,7 @@
             jax.ShapeDtypeStruct((3, FT, CELLS), F32),
             jax.ShapeDtypeStruct((4, NP, EL), F32),
         ),
-        in_specs=[any_space] * 12,
+        in_specs=[hbm] * 12,
         out_specs=(any_space,) * 3,
         scratch_shapes=[
             pltpu.VMEM((5, WIDE, CELLS), F32),
@@ -483,8 +495,8 @@
             pltpu.VMEM((TURNS, 4 * NP, EL), BF16),
             pltpu.VMEM((TURNS, 4 * NP, 128), BF16),
             pltpu.VMEM((TURNS, 4 * NP, 128), BF16),
-            pltpu.VMEM((6, EL), jnp.int32),
-            pltpu.VMEM((6, EL), jnp.int32),
+            pltpu.VMEM((6, 1, EL), jnp.int32),
+            pltpu.VMEM((6, 1, EL), jnp.int32),
             pltpu.VMEM((192, 192), BF16),
             pltpu.VMEM((96, NP), BF16),
             pltpu.VMEM((NP, 384), BF16),
@@ -502,7 +514,21 @@
         compiler_params=pltpu.CompilerParams(
             collective_id=0, has_side_effects=True, vmem_limit_bytes=48 * 1024 * 1024
         ),
-    )(ff[0], mv[0], cv[0], tl[0], tt, pj, ac[0], en[0], fc[0], *constants())
+    )(*(
+        pltpu.with_memory_space_constraint(x, pltpu.MemorySpace.HBM)
+        for x in (
+            ff[0], mv[0], cv[0], tl[0], tt, pj, ac[0],
+            jnp.swapaxes(en, 0, 1), jnp.swapaxes(fc, 0, 1), *constants(),
+        )
+    ))
+    outs = pl.pallas_call(
+        store,
+        out_shape=tuple(jax.ShapeDtypeStruct(o.shape, o.dtype) for o in outs),
+        in_specs=[any_space] * 3,
+        out_specs=(hbm,) * 3,
+        scratch_shapes=[dma((3,))],
+        compiler_params=pltpu.CompilerParams(vmem_limit_bytes=1024 * 1024),
+    )(*outs)
     return tuple(o[None] for o in outs)
 
 

time: 42.1 us -> 33 us (0.78); the launches traced: 41.6 us -> 32.9 us
  local copies, waits for them, and re-layouts: 10.1 us -> 0 us
  Pallas kernels: 30.9 us -> 32.3 us
    unnamed x24 -> x0, local copies, waits for them, and re-layouts: 10.1 us -> none
    pallas_call x0 -> x1, Pallas kernels: none -> 1.08 us  [body(): pl.pallas_call(store, out_shape=tuple((jax.ShapeDtypeStruct(o.shape, o.dt...]
where the time goes in v2:
time: 33 us; the launch traced here: 32.9 us
  Pallas kernels  32.3 us (98%)
  between operations  0.64 us (2%)
    pallas_call x1, Pallas kernels, body(): pl.pallas_call(functools.partial(kernel, n_sfc), out_shape=(jax.ShapeDtyp...  31.2 us
    pallas_call x1, Pallas kernels, body(): pl.pallas_call(store, out_shape=tuple((jax.ShapeDtypeStruct(o.shape, o.dt...  1.08 us

profile of v2, /device:TPU:24, one launch (start us, length us, event | category | flops | bytes accessed | tf_op | source)
XLA Modules:
  0.0 32.9 jit_solution(2147583489372235392)
XLA Ops:
  0.6 31.2 %shard_map.139 = (f32[5,256,128]{2,1,0:T(8,128)S(1)}, f32[3,256,128]{2,1,0:T(8,128)S(1)}, f32[4,64,256]{2,1,0:T(8,128)S(1)}) custom-call(f32[5,256,128]{2,1,0:T(8,128)} %bitcast.10, f32[3,256,128]{2,1,0:T(8,128)} %bitcast.11, f32[256,128]{1,0:T(8,128)} %bitcast.13, s32[4,256]{1,0:T(4,128)} %bitcast.16, s32[1,256]{1,0:T(1,128)} %tt.1, f32[64,128]{1,0:T(8,128)} %pj.1, ...), custom_call_target="tpu_custom_call" | custom-call | tf_op jit(solution)/shard_map/pallas_call | solution.py:471
  31.8 1.1 %shard_map.140 = (f32[5,256,128]{2,1,0:T(8,128)}, f32[3,256,128]{2,1,0:T(8,128)}, f32[4,64,256]{2,1,0:T(8,128)}) custom-call(f32[5,256,128]{2,1,0:T(8,128)S(1)} %get-tuple-element.9.a, f32[3,256,128]{2,1,0:T(8,128)S(1)} %get-tuple-element.10.b, f32[4,64,256]{2,1,0:T(8,128)S(1)} %get-tuple-element.11.c), custom_call_target="tpu_custom_call" | custom-call | tf_op jit(solution)/shard_map/pallas_call | solution.py:524

commit v3 on v2

v3 whole, which is shorter than its diff:
```python
import functools

import jax
import jax.numpy as jnp
import numpy as np
from jax import lax
from jax.experimental import pallas as pl
from jax.experimental.pallas import tpu as pltpu
from jax.sharding import PartitionSpec as P

MESH = pl.DeviceIdType.MESH
F32 = jnp.float32
BF16 = jnp.bfloat16

HW = 16
FT = 256
CELLS = 128
HALO = 3 * HW
WIDE = FT + 2 * HALO
EL = 256
NP = 64
TURNS = 2
SHARE = 128
ROUTE = {(0, 1): "direct", (0, 0): "direct", (1, 1): "direct", (1, 0): "direct"}


def derivative_operators():
    points = np.array([-1.0, -1.0 / np.sqrt(5.0), 1.0 / np.sqrt(5.0), 1.0])
    weights = np.array(
        [
            1.0 / np.prod([points[col] - points[other] for other in range(4) if other != col])
            for col in range(4)
        ]
    )
    matrix = np.zeros((4, 4))
    for line in range(4):
        for col in range(4):
            if line != col:
                matrix[line, col] = weights[col] / weights[line] / (points[line] - points[col])
        matrix[line, line] = -matrix[line].sum()
    eye = np.eye(4)
    return np.concatenate(
        [
            np.kron(eye, np.kron(eye, matrix)),
            np.kron(eye, np.kron(matrix, eye)),
            np.kron(matrix, np.kron(eye, eye)),
        ]
    ).astype(np.float32)


def face_tables():
    faces = []
    for face in range(6):
        axis, level = face // 2, 3 * (face % 2)
        members = []
        for second in range(4):
            for first in range(4):
                coords = [first, second]
                coords.insert(axis, level)
                members.append(coords[0] + 4 * coords[1] + 16 * coords[2])
        faces.append(members)
    turns = []
    for turn in range(4):
        mapping = []
        for second in range(4):
            for first in range(4):
                source = ((first, second), (3 - second, first), (3 - first, 3 - second), (second, 3 - first))[turn]
                mapping.append(source[0] + 4 * source[1])
        turns.append(mapping)
    return faces, turns


def constants():
    deriv = jnp.asarray(derivative_operators())
    high = deriv.astype(BF16)
    low = (deriv - high.astype(F32)).astype(BF16)
    deriv3 = jnp.concatenate([high, high, low], 1)
    faces, turns = face_tables()
    pick = np.zeros((96, NP), np.float32)
    put = np.zeros((NP, 4 * 96), np.float32)
    for face in range(6):
        for p in range(16):
            pick[16 * face + p, faces[face ^ 1][p]] = 1
            for turn in range(4):
                put[faces[face][p], 96 * turn + 16 * face + turns[turn][p]] = 1
    return deriv3, jnp.asarray(pick, BF16), jnp.asarray(put, BF16)


def halves(x):
    high = x.astype(BF16)
    return high, (x - high.astype(F32)).astype(BF16)


def dot(a, b):
    return lax.dot_general(a, b, (((1,), (0,)), ((), ())), preferred_element_type=F32)


def dot_t(a, b):
    return lax.dot_general(a, b, (((1,), (1,)), ((), ())), preferred_element_type=F32)


def kernel(
    n_sfc,
    ff, mv, cv, tl, tt, pj, ac, en, fc, d3_h, pick_h, put_h,
    fo, mo, ao,
    w0, w1, vis, hb, hn, lk, mean, sel_mid, sel_end, xb, pay, tgt, oht, ohn, pb, away, came, tot, res, proj,
    st, sb, ends, hl, hr, enb, fcb, d3, pick, put, ohf, grad, src,
    ls, hs, hrs, ts, trs, ps, prs, ns, nrs, rs, rrs, as_, ars, outs,
):
    g = lax.axis_index("grp")
    s = lax.axis_index("sfc")
    right = lax.rem(s + 1, n_sfc)
    left = lax.rem(s + n_sfc - 1, n_sfc)
    first = s * FT
    has_left = s > 0
    has_right = s < n_sfc - 1
    barrier = pltpu.get_barrier_semaphore()

    def greet(gg, ss):
        pl.semaphore_signal(barrier, inc=1, device_id=(gg, ss), device_id_type=MESH)

    for d in (1, 2, 3):
        greet(lax.rem(g + d, 4), s)
    for there, ss in ((has_right, right), (has_left, left)):

        @pl.when(there)
        def _():
            greet(g, ss)

    inside = jnp.logical_and(has_left, has_right)

    def meet():
        pl.when(inside)(lambda: pl.semaphore_wait(barrier, 5))
        pl.when(jnp.logical_not(inside))(lambda: pl.semaphore_wait(barrier, 4))

    class Pair:
        def __init__(self, to_left, to_right):
            self.to_left, self.to_right = to_left, to_right

        def start(self):
            pl.when(has_left)(self.to_left.start)
            pl.when(has_right)(self.to_right.start)

        def wait_recv(self):
            pl.when(has_right)(self.to_left.wait_recv)
            pl.when(has_left)(self.to_right.wait_recv)

        def wait_send(self):
            pl.when(has_left)(self.to_left.wait_send)
            pl.when(has_right)(self.to_right.wait_send)

    def load(source, target, k):
        copy = pltpu.make_async_copy(source, target, ls.at[k])
        copy.start()
        return copy

    def remote(source, target, send, recv, gg, ss):
        return pltpu.make_async_remote_copy(
            src_ref=source, dst_ref=target, send_sem=send, recv_sem=recv,
            device_id=(gg, ss), device_id_type=MESH,
        )

    load_state = load(ff, w0.at[:, HALO : HALO + FT, :], 0)
    load_mean = load(mv, mean, 1)
    load_sound = load(ac, st, 2)

    odd = lax.rem(s, 2) == 1
    even = jnp.logical_not(odd)
    direct_out = {"direct": has_right, "mixed": jnp.logical_and(odd, has_right)}
    direct_in = {"direct": has_left, "mixed": jnp.logical_and(even, has_left)}
    relay_out = {"relay": has_right, "mixed": even}
    relay_in = {"relay": has_left, "mixed": odd}
    mine = pl.ds(pl.multiple_of(SHARE * g, SHARE), SHARE)

    def target(d, h):
        return remote(
            tt, tgt.at[h, g], ts.at[h, d], trs.at[h, g], lax.rem(g + d, 3), right if h else s
        )

    def target_from(q, h):
        return remote(tt, tgt.at[h, q], ts.at[h, 0], trs.at[h, q], lax.rem(g + 1, 3), s)

    def block(turn, part, d, h):
        w = lax.rem(g + d, 3)
        return remote(
            pay.at[turn, part, pl.ds(pl.multiple_of(SHARE * w, SHARE), SHARE), :],
            pb.at[turn, part, h, g], ps.at[turn, part, h, d], prs.at[turn, part, h, g],
            w, right if h else s,
        )

    def block_from(turn, part, q, h):
        return remote(
            pay.at[turn, part, 0:SHARE, :], pb.at[turn, part, h, q],
            ps.at[turn, part, h, 0], prs.at[turn, part, h, q], lax.rem(g + 1, 3), s,
        )

    def passed(turn, part):
        return remote(
            away.at[turn, part], came.at[turn, part],
            ns.at[turn, part], nrs.at[turn, part], g, right,
        )

    def blank_targets():
        @pl.when(jnp.logical_not(has_left))
        def _():
            for q in range(3):
                tgt[1, q] = jnp.full((1, FT), -1, jnp.int32)

    def hot_targets():
        for q in range(3):
            pl.when(g != q)(target_from(q, 0).wait_recv)

        @pl.when(has_left)
        def _():
            for q in range(3):
                target_from(q, 1).wait_recv()

        element = lax.broadcasted_iota(jnp.int32, (EL, FT), 0) + s * EL
        count = jnp.zeros((16, EL), F32)
        ones = jnp.ones((16, FT), BF16)
        for h in range(2):
            for q in range(3):
                order = pltpu.roll(jnp.broadcast_to(tgt[h, q], (8, FT)), 64, 1)[0:1]
                hot = jnp.where(order == element, F32(1.0), F32(0.0)).astype(BF16)
                oht[h, q] = hot
                count = count + dot_t(ones, hot)
                if h == 0:
                    ohn[q] = jnp.where(order == element + EL, F32(1.0), F32(0.0)).astype(BF16)
        return 1.0 / jnp.maximum(count[0:1], 1.0)

    def pass_on(turn, part):
        if ROUTE[turn, part] == "direct":
            return

        @pl.when(relay_out[ROUTE[turn, part]])
        def _():
            cols = slice(128 * part, 128 * part + 128)
            total = sum(dot_t(pb[turn, part, 0, q], ohn[q, :, cols]) for q in range(3))
            away[turn, part] = total.astype(BF16)
            passed(turn, part).start()

    def reduce(turn, inverse):
        for part in (1, 0):
            for q in range(3):
                pl.when(g != q)(block_from(turn, part, q, 0).wait_recv)
            pass_on(turn, part)
        total = jnp.zeros((SHARE, EL), F32)
        for q in range(3):
            total = total + dot_t(
                jnp.concatenate([pb[turn, 0, 0, q], pb[turn, 1, 0, q]], 1), oht[0, q]
            )
        tot[...] = total
        for part in (1, 0):
            route = ROUTE[turn, part]
            if route != "relay":

                @pl.when(direct_in[route])
                def _():
                    more = jnp.zeros((SHARE, EL), F32)
                    for q in range(3):
                        block_from(turn, part, q, 1).wait_recv()
                        cols = slice(128 * part, 128 * part + 128)
                        more = more + dot_t(pb[turn, part, 1, q], oht[1, q, :, cols])
                    tot[...] += more

            if route != "direct":

                @pl.when(relay_in[route])
                def _():
                    passed(turn, part).wait_recv()
                    tot[...] += came[turn, part].astype(F32)

        return (tot[...] * inverse).astype(BF16)

    def passed_sent():
        for (turn, part), route in ROUTE.items():
            if route != "direct":
                pl.when(relay_out[route])(passed(turn, part).wait_send)

    @pl.when(g < 3)
    def _():
        load_visc = load(cv, vis.at[HALO : HALO + FT, :], 3)
        load_links = load(tl, lk.at[0:4, 128 : 128 + FT], 4)
        load_targets = load(tt, tgt.at[0, g], 5)
        load_proj = load(pj, proj, 6)
        load_state.wait()
        load_visc.wait()
        for side, at in ((0, HALO), (1, FT)):
            for f in range(5):
                hb[side, f] = w0[f, at : at + HALO, :].astype(BF16)
            hb[side, 5] = vis[at : at + HALO, :].astype(BF16)
        meet()
        halo = Pair(
            remote(hb.at[0], hn.at[1], hs.at[0], hrs.at[0], g, left),
            remote(hb.at[1], hn.at[0], hs.at[1], hrs.at[1], g, right),
        )
        halo_links = Pair(
            remote(tl.at[:, 0:128], lk.at[0:4, 128 + FT : 256 + FT], hs.at[2], hrs.at[2], g, left),
            remote(tl.at[:, FT - 128 : FT], lk.at[0:4, 0:128], hs.at[3], hrs.at[3], g, right),
        )
        halo.start()
        halo_links.start()
        for there, slot, lanes in ((has_left, 0, slice(0, 128)), (has_right, 1, slice(128 + FT, 256 + FT))):

            @pl.when(jnp.logical_not(there))
            def _():
                hn[slot] = jnp.zeros((6, HALO, CELLS), BF16)
                lk[0:4, lanes] = jnp.zeros((4, 128), jnp.int32)

        for d in (1, 2):
            target(d, 0).start()
        blank_targets()
        lk[4:8, :] = jnp.zeros((4, 2 * 128 + FT), jnp.int32)
        blank = jnp.zeros((HW, CELLS), F32)
        for f in range(5):
            for at in (0, HALO, HALO + FT - HW, WIDE - HW):
                w1[f, at : at + HW, :] = blank

        def select(links, own, shift):
            cols = lax.broadcasted_iota(jnp.int32, (links.shape[0], 256), 1)
            hot = []
            for k in range(4):
                link = links[:, k : k + 1]
                at = jnp.where(link < 0, own, link - shift)
                hot.append(jnp.where(cols == at, F32(1.0), F32(0.0)))
            return (
                (hot[0] + hot[1] + hot[2] + hot[3]).astype(BF16),
                (hot[0] - hot[1]).astype(BF16),
                (hot[2] - hot[3]).astype(BF16),
            )

        def rows_at(ref, k, ranges):
            parts = [ref[k, i:j, :] for i, j in ranges]
            return parts[0] if len(parts) == 1 else jnp.concatenate(parts, 0)

        def gather(rows, window):
            r = dot(rows, jnp.concatenate(halves(window), 1))
            return r[:, :CELLS] + r[:, CELLS:]

        def east_west(c):
            return pltpu.roll(c, CELLS - 1, 1), pltpu.roll(c, 1, 1)

        def advance(source, target, rows, columns, ranges, fields):
            n = sum(j - i for i, j in ranges)
            nu = jnp.concatenate([vis[i:j, :] for i, j in ranges], 0)
            velocity = [rows_at(source, f, ranges) for f in (1, 2, 3)]
            differences = []
            for f in fields:
                c = velocity[f - 1] if 0 < f < 4 else rows_at(source, f, ranges)
                near = gather(rows, rows_at(source, f, columns))
                around, d2, d3_ = near[0:n], near[n : 2 * n], near[2 * n : 3 * n]
                east, west = east_west(c)
                d1 = east - west
                new = (
                    c
                    + nu * (east + west + around - 6.0 * c)
                    - 0.05 * (velocity[0] * d1 + velocity[1] * d2 + velocity[2] * d3_)
                )
                at = 0
                for i, j in ranges:
                    target[f, i:j, :] = new[at : at + j - i]
                    at += j - i
                differences.append((d1, d2, d3_))
            return velocity, differences

        def differ(source, rows, columns, ranges):
            n = sum(j - i for i, j in ranges)
            velocity, differences = [], []
            for f in (1, 2, 3):
                c = rows_at(source, f, ranges)
                near = gather(rows, rows_at(source, f, columns))
                east, west = east_west(c)
                velocity.append(c)
                differences.append((east - west, near[0:n], near[n : 2 * n]))
            return velocity, differences

        def sources(turn, own, velocity, differences):
            (u1, u2, u3), (v1, v2, v3), (w1_, w2_, w3_) = differences
            u, v, w = velocity
            vx = 0.5 * (w2_ - v3)
            vy = 0.5 * (u3 - w1_)
            vz = 0.5 * (v1 - u2)
            packed = [vy * w - vz * v, vz * u - vx * w, vx * v - vy * u]
            for k in range(3):
                m = 0.9 * rows_at(mean, k, own) + 0.1 * velocity[k]
                packed.append(m)
                at = 0
                for i, j in own:
                    mean[k, i:j, :] = m[at : at + j - i]
                    at += j - i
            for k in range(6):
                hi, lo = halves(packed[k])
                at = 0
                for i, j in own:
                    for part, base, x0, x1 in ((0, 64, 0, 64), (1, -64, 64, 192), (0, -192, 192, 256)):
                        lo_, hi_ = max(i, x0), min(j, x1)
                        if lo_ < hi_:
                            rows = slice(at + lo_ - i, at + hi_ - i)
                            to = slice(lo_ + base, hi_ + base)
                            xb[turn, part, k, to, 0:128] = hi[rows]
                            xb[turn, part, k, to, 128:256] = lo[rows]
                    at += j - i

        def project(turn, part):
            for k in range(6):
                x = xb[turn, part, k]
                pay[turn, part, NP * k : NP * (k + 1), :] = (
                    dot_t(p2, x) + dot_t(plow, x[:, 0:128])
                ).astype(BF16)
            pb[turn, part, 0, g] = pay[turn, part, mine, :]

        def send_payload(turn, part):
            for d in (1, 2):
                block(turn, part, d, 0).start()

        def send_next(turn, part):
            if ROUTE[turn, part] != "relay":

                @pl.when(direct_out[ROUTE[turn, part]])
                def _():
                    for d in (1, 2, 0):
                        block(turn, part, d, 1).start()

        load_links.wait()
        mid = HALO + HW, HALO + FT - HW
        n_mid = FT - 2 * HW
        own = lax.broadcasted_iota(jnp.int32, (n_mid, 1), 0) + HW
        links = jnp.transpose(lk[:, 128 : 128 + FT])[HW : FT - HW]
        for m, hot in enumerate(select(links, own, first)):
            sel_mid[m] = hot
        load_proj.wait()
        load_mean.wait()
        ph, plow = halves(proj[...])
        p2 = jnp.concatenate([ph, ph], 1)

        def mid_rows(skip, mats):
            return jnp.concatenate([sel_mid[m, skip : n_mid - skip, :] for m in mats], 0)

        inner = [(HALO, HALO + FT)]
        advance(w0, w1, mid_rows(0, (0, 1, 2)), inner, [mid], (0, 1, 2, 3, 4))
        one = [(mid[0] + HW, mid[1] - HW)]
        velocity, differences = advance(w1, w0, mid_rows(HW, (0, 1, 2)), inner, one, (1, 2, 3))
        sources(0, [(2 * HW, FT - 2 * HW)], velocity, differences)
        project(0, 1)
        send_payload(0, 1)
        two = [(mid[0] + 2 * HW, mid[1] - 2 * HW)]
        velocity, differences = differ(w0, mid_rows(2 * HW, (1, 2)), inner, two)
        sources(1, [(3 * HW, FT - 3 * HW)], velocity, differences)
        project(1, 1)

        halo_links.wait_recv()

        @pl.when(has_right)
        def _():
            for d in range(3):
                target(d, 1).start()

        send_next(0, 1)
        n_end = 5 * HW
        place = lax.broadcasted_iota(jnp.int32, (n_end, 1), 0)
        lt = jnp.transpose(lk[...])
        for side, (at, own_at, shift) in enumerate(
            ((128 - 2 * HW, HW, first - HALO), (128 + FT - HALO, 128 + 2 * HW, first + HALO))
        ):
            for m, hot in enumerate(select(lt[at : at + n_end], place + own_at, shift)):
                sel_end[m, n_end * side : n_end * (side + 1), :] = hot
        halo.wait_recv()
        for side, at in ((0, 0), (1, HALO + FT)):
            for f in range(5):
                w0[f, at : at + HALO, :] = hn[side, f].astype(F32)
            vis[at : at + HALO, :] = hn[side, 5].astype(F32)

        def end_rows(skip, mats):
            parts = []
            for m in mats:
                parts.append(sel_end[m, skip : skip + HALO, :])
                parts.append(sel_end[m, 2 * n_end - HALO - skip : 2 * n_end - skip, :])
            return jnp.concatenate(parts, 0)

        outer = [(0, 128), (WIDE - 128, WIDE)]

        def end_ranges(skip):
            return [(skip, skip + HALO), (WIDE - HALO - skip, WIDE - skip)]

        advance(w0, w1, end_rows(0, (0, 1, 2)), outer, end_ranges(HW), (1, 2, 3, 0, 4))
        velocity, differences = advance(
            w1, w0, end_rows(HW, (0, 1, 2)), outer, end_ranges(2 * HW), (1, 2, 3)
        )
        sources(
            0,
            [(0, 2 * HW), (FT - 2 * HW, FT)],
            [x[HW : HW + 4 * HW] for x in velocity],
            [[x[HW : HW + 4 * HW] for x in d] for d in differences],
        )
        project(0, 0)
        send_payload(0, 0)
        send_next(0, 0)
        send_payload(1, 1)
        send_next(1, 1)
        velocity, differences = differ(w0, end_rows(2 * HW, (1, 2)), outer, end_ranges(3 * HW))
        sources(1, [(0, 3 * HW), (FT - 3 * HW, FT)], velocity, differences)
        project(1, 0)
        send_payload(1, 0)
        send_next(1, 0)
        load_targets.wait()
        inverse = hot_targets()
        for turn in range(TURNS):
            res[turn] = reduce(turn, inverse)
            remote(
                res.at[turn], src.at[turn, mine, :], rs.at[turn], rrs.at[turn, g], 3, s
            ).start()
        advance(w1, w0, mid_rows(HW, (0, 1, 2)), inner, one, (0, 4))
        advance(w1, w0, end_rows(HW, (0, 1, 2)), outer, end_ranges(2 * HW), (0, 4))
        load_sound.wait()
        writes = [
            pltpu.make_async_copy(w0.at[:, HALO : HALO + FT, :], fo, outs.at[0]),
            pltpu.make_async_copy(mean, mo, outs.at[1]),
            pltpu.make_async_copy(st, ao, outs.at[2]),
        ]
        for copy in writes:
            copy.start()

        for turn in range(TURNS):
            remote(
                res.at[turn], src.at[turn, mine, :], rs.at[turn], rrs.at[turn, g], 3, s
            ).wait_send()
            for part in range(2):
                route = ROUTE[turn, part]
                for d in (1, 2):
                    block(turn, part, d, 0).wait_send()
                if route != "relay":

                    @pl.when(direct_out[route])
                    def _():
                        for d in range(3):
                            block(turn, part, d, 1).wait_send()

        passed_sent()
        for d in (1, 2):
            target(d, 0).wait_send()

        @pl.when(has_right)
        def _():
            for d in range(3):
                target(d, 1).wait_send()

        halo.wait_send()
        halo_links.wait_send()
        for copy in writes:
            copy.wait()

    @pl.when(g == 3)
    def _():
        loads = [
            load(en, enb, 3),
            load(fc, fcb, 4),
            load(d3_h, d3, 5),
            load(pick_h, pick, 6),
            load(put_h, put, 7),
        ]
        meet()
        load_sound.wait()

        def send_state(turn):
            for side, at, lanes in ((0, 0, slice(0, 128)), (1, 112, slice(128, 256))):
                packed = jnp.zeros((32, 128), F32)
                for q in range(8):
                    x = st[q // 2, 32 * (q % 2) : 32 * (q % 2) + 32, lanes]
                    packed = jnp.where(group == q, pltpu.roll(x, (HW * q - at) % 128, 1), packed)
                ends[turn, side] = packed.astype(BF16)
            copies = Pair(
                remote(ends.at[turn, 0], hr.at[turn], as_.at[turn, 0], ars.at[turn, 0], 3, left),
                remote(ends.at[turn, 1], hl.at[turn], as_.at[turn, 1], ars.at[turn, 1], 3, right),
            )
            copies.start()
            for there, box in ((has_left, hl), (has_right, hr)):

                @pl.when(jnp.logical_not(there))
                def _():
                    box[turn] = jnp.zeros((32, 128), BF16)

            for v in range(4):
                sb[turn, NP * v : NP * (v + 1), :] = st[v].astype(BF16)
            return copies

        group = lax.broadcasted_iota(jnp.int32, (32, 128), 1) >> 4
        sends = send_state(0)
        load_state.wait()
        load_mean.wait()
        writes = [
            pltpu.make_async_copy(w0.at[:, HALO : HALO + FT, :], fo, outs.at[0]),
            pltpu.make_async_copy(mean, mo, outs.at[1]),
        ]
        for copy in writes:
            copy.start()
        for copy in loads:
            copy.wait()

        row = lax.broadcasted_iota(jnp.int32, (EL + 128, EL), 0)
        for f in range(6):
            link = enb[f]
            at = link - s * EL
            at = jnp.where(link < 0, 999, jnp.where(at < 0, at + (EL + 128), at))
            ohf[f] = jnp.where(row == at, F32(1.0), F32(0.0)).astype(BF16)
        node = lax.broadcasted_iota(jnp.int32, (NP, EL), 0)
        faces_on = jnp.zeros((NP, EL), F32)
        for f in range(6):
            coordinate = (node >> (2 * (f // 2))) & 3
            valid = jnp.where(enb[f] >= 0, F32(1.0), F32(0.0))
            faces_on = faces_on + jnp.where(coordinate == 3 * (f % 2), valid, F32(0.0))

        for turn in range(TURNS):
            for v in range(4):
                hi, lo = halves(st[v])
                grad[v] = dot(d3[...], jnp.concatenate([hi, lo, hi], 0))
            sends.wait_recv()
            sends.wait_send()
            after, before_ = hr[turn].astype(F32), hl[turn].astype(F32)
            beside = jnp.concatenate(
                [
                    jnp.where(
                        group == 0,
                        pltpu.roll(after, (-HW * q) % 128, 1),
                        pltpu.roll(before_, (112 - HW * q) % 128, 1),
                    )
                    for q in range(8)
                ],
                0,
            ).astype(BF16)
            facing = []
            for v in range(4):
                rows = slice(NP * v, NP * (v + 1))
                wide = jnp.concatenate([sb[turn, rows, :], beside[rows]], 1)
                facing.append(dot(pick[...], wide).astype(BF16))
            remotes = []
            for f in range(6):
                stacked = jnp.concatenate([facing[v][16 * f : 16 * f + 16] for v in range(4)], 0)
                remotes.append(dot(stacked, ohf[f]))
            before = []
            for v in range(4):
                turned = []
                for r in range(4):
                    for f in range(6):
                        turned.append(
                            jnp.where(
                                fcb[f] == r, remotes[f][16 * v : 16 * v + 16], F32(0.0)
                            ).astype(BF16)
                        )
                jump = dot(put[...], jnp.concatenate(turned, 0)) - faces_on * st[v]
                if v == 0:
                    linear = grad[1, 0:64] + grad[2, 64:128] + grad[3, 128:192]
                else:
                    linear = grad[0, 64 * (v - 1) : 64 * v]
                before.append(st[v] + 0.08 * (1.5 * jump - linear))
            for w in range(3):
                rows = slice(SHARE * w, SHARE * w + SHARE)
                remote(
                    res.at[turn], src.at[turn, rows, :], rs.at[turn], rrs.at[turn, w], w, s
                ).wait_recv()
            flow = [src[turn, 192 + 64 * d : 256 + 64 * d, :].astype(F32) for d in range(3)]
            for v in range(4):
                convect = sum(flow[d] * grad[v, 64 * d : 64 * d + 64] for d in range(3))
                if v:
                    convect = convect + src[turn, 64 * (v - 1) : 64 * v, :].astype(F32)
                st[v] = before[v] - 0.08 * convect
            if turn == 0:
                sends = send_state(1)
        write = pltpu.make_async_copy(st, ao, outs.at[2])
        write.start()
        for copy in writes:
            copy.wait()
        write.wait()


def store(a, b, c, x, y, z, sems):
    copies = [
        pltpu.make_async_copy(source, target, sems.at[k])
        for k, (source, target) in enumerate(((a, x), (b, y), (c, z)))
    ]
    for copy in copies:
        copy.start()
    for copy in copies:
        copy.wait()


def body(ff, mv, cv, tl, tt, pj, ac, en, fc):
    n_sfc = lax.axis_size("sfc")
    hbm = pl.BlockSpec(memory_space=pltpu.MemorySpace.HBM)
    any_space = pl.BlockSpec(memory_space=pl.ANY)
    dma = pltpu.SemaphoreType.DMA
    outs = pl.pallas_call(
        functools.partial(kernel, n_sfc),
        out_shape=(
            jax.ShapeDtypeStruct((5, FT, CELLS), F32),
            jax.ShapeDtypeStruct((3, FT, CELLS), F32),
            jax.ShapeDtypeStruct((4, NP, EL), F32),
        ),
        in_specs=[hbm] * 12,
        out_specs=(any_space,) * 3,
        scratch_shapes=[
            pltpu.VMEM((5, WIDE, CELLS), F32),
            pltpu.VMEM((5, WIDE, CELLS), F32),
            pltpu.VMEM((WIDE, CELLS), F32),
            pltpu.VMEM((2, 6, HALO, CELLS), BF16),
            pltpu.VMEM((2, 6, HALO, CELLS), BF16),
            pltpu.VMEM((8, 256 + FT), jnp.int32),
            pltpu.VMEM((3, FT, CELLS), F32),
            pltpu.VMEM((3, FT - 2 * HW, 256), BF16),
            pltpu.VMEM((3, 10 * HW, 256), BF16),
            pltpu.VMEM((TURNS, 2, 6, 128, 256), BF16),
            pltpu.VMEM((TURNS, 2, 6 * NP, 128), BF16),
            pltpu.VMEM((2, 3, 1, FT), jnp.int32),
            pltpu.VMEM((2, 3, EL, FT), BF16),
            pltpu.VMEM((3, EL, FT), BF16),
            pltpu.VMEM((TURNS, 2, 2, 3, SHARE, 128), BF16),
            pltpu.VMEM((TURNS, 2, SHARE, EL), BF16),
            pltpu.VMEM((TURNS, 2, SHARE, EL), BF16),
            pltpu.VMEM((SHARE, EL), F32),
            pltpu.VMEM((TURNS, SHARE, EL), BF16),
            pltpu.VMEM((NP, CELLS), F32),
            pltpu.VMEM((4, NP, EL), F32),
            pltpu.VMEM((TURNS, 4 * NP, EL), BF16),
            pltpu.VMEM((TURNS, 2, 32, 128), BF16),
            pltpu.VMEM((TURNS, 32, 128), BF16),
            pltpu.VMEM((TURNS, 32, 128), BF16),
            pltpu.VMEM((6, 1, EL), jnp.int32),
            pltpu.VMEM((6, 1, EL), jnp.int32),
            pltpu.VMEM((192, 192), BF16),
            pltpu.VMEM((96, NP), BF16),
            pltpu.VMEM((NP, 384), BF16),
            pltpu.VMEM((6, EL + 128, EL), BF16),
            pltpu.VMEM((4, 192, EL), F32),
            pltpu.VMEM((TURNS, 6 * NP, EL), BF16),
            dma((8,)),
            dma((4,)), dma((4,)),
            dma((2, 3)), dma((2, 3)),
            dma((TURNS, 2, 2, 3)), dma((TURNS, 2, 2, 3)),
            dma((TURNS, 2)), dma((TURNS, 2)),
            dma((TURNS,)), dma((TURNS, 3)),
            dma((TURNS, 2)), dma((TURNS, 2)),
            dma((3,)),
        ],
        compiler_params=pltpu.CompilerParams(
            collective_id=0, has_side_effects=True, vmem_limit_bytes=48 * 1024 * 1024
        ),
    )(*(
        pltpu.with_memory_space_constraint(x, pltpu.MemorySpace.HBM)
        for x in (
            ff[0], mv[0], cv[0], tl[0], tt, pj, ac[0],
            jnp.swapaxes(en, 0, 1), jnp.swapaxes(fc, 0, 1), *constants(),
        )
    ))
    outs = pl.pallas_call(
        store,
        out_shape=tuple(jax.ShapeDtypeStruct(o.shape, o.dtype) for o in outs),
        in_specs=[any_space] * 3,
        out_specs=(hbm,) * 3,
        scratch_shapes=[dma((3,))],
        compiler_params=pltpu.CompilerParams(vmem_limit_bytes=1024 * 1024),
    )(*outs)
    return tuple(o[None] for o in outs)


def solution(mesh):
    placed = (
        P("grp", None, "sfc", None),
        P("grp", None, "sfc", None),
        P("grp", "sfc", None),
        P("grp", None, "sfc"),
        P("grp", "sfc"),
        P(),
        P("grp", None, None, "sfc"),
        P("grp", None, "sfc"),
        P("grp", None, "sfc"),
    )
    return jax.shard_map(
        body,
        mesh=mesh,
        in_specs=placed,
        out_specs=(
            P("grp", None, "sfc", None),
            P("grp", None, "sfc", None),
            P("grp", None, None, "sfc"),
        ),
        check_vma=False,
    )
```

time: 33 us -> 25.1 us (0.76)
  the two profiles are of different devices: /device:TPU:24 before, /device:TPU:56 now
where the time goes in v3:
time: 25.1 us; the launch traced here: 25 us
  Pallas kernels  24.3 us (97%)
  between operations  0.64 us (3%)
    pallas_call x1, Pallas kernels, body(): pl.pallas_call(functools.partial(kernel, n_sfc), out_shape=(jax.ShapeDtyp...  23.3 us
    pallas_call x1, Pallas kernels, body(): pl.pallas_call(store, out_shape=tuple((jax.ShapeDtypeStruct(o.shape, o.dt...  1.08 us

profile of v3, /device:TPU:56, one launch (start us, length us, event | category | flops | bytes accessed | tf_op | source)
XLA Modules:
  0.0 25.0 jit_solution(17719258145288709530)
XLA Ops:
  0.6 23.3 %shard_map.139 = (f32[5,256,128]{2,1,0:T(8,128)S(1)}, f32[3,256,128]{2,1,0:T(8,128)S(1)}, f32[4,64,256]{2,1,0:T(8,128)S(1)}) custom-call(f32[5,256,128]{2,1,0:T(8,128)} %bitcast.10, f32[3,256,128]{2,1,0:T(8,128)} %bitcast.11, f32[256,128]{1,0:T(8,128)} %bitcast.13, s32[4,256]{1,0:T(4,128)} %bitcast.16, s32[1,256]{1,0:T(1,128)} %tt.1, f32[64,128]{1,0:T(8,128)} %pj.1, ...), custom_call_target="tpu_custom_call" | custom-call | tf_op jit(solution)/shard_map/pallas_call | solution.py:691
  23.9 1.1 %shard_map.140 = (f32[5,256,128]{2,1,0:T(8,128)}, f32[3,256,128]{2,1,0:T(8,128)}, f32[4,64,256]{2,1,0:T(8,128)}) custom-call(f32[5,256,128]{2,1,0:T(8,128)S(1)} %get-tuple-element.9.a, f32[3,256,128]{2,1,0:T(8,128)S(1)} %get-tuple-element.10.b, f32[4,64,256]{2,1,0:T(8,128)S(1)} %get-tuple-element.11.c), custom_call_target="tpu_custom_call" | custom-call | tf_op jit(solution)/shard_map/pallas_call | solution.py:753

commit v4 on v3

--- a/solution.py
+++ b/solution.py
@@ -21,7 +21,7 @@
 NP = 64
 TURNS = 2
 SHARE = 128
-ROUTE = {(0, 1): "direct", (0, 0): "direct", (1, 1): "direct", (1, 0): "direct"}
+ROUTE = {(0, 1): "direct", (0, 0): "direct", (1, 1): "mixed", (1, 0): "direct"}
 
 
 def derivative_operators():
@@ -102,9 +102,9 @@
 def kernel(
     n_sfc,
     ff, mv, cv, tl, tt, pj, ac, en, fc, d3_h, pick_h, put_h,
-    fo, mo, ao,
-    w0, w1, vis, hb, hn, lk, mean, sel_mid, sel_end, xb, pay, tgt, oht, ohn, pb, away, came, tot, res, proj,
-    st, sb, ends, hl, hr, enb, fcb, d3, pick, put, ohf, grad, src,
+    fo, mean, st,
+    w0, w1, w2, vis, hb, hn, lk, sel_mid, sel_end, xb, pay, tgt, oht, ohn, pb, away, came, tot, res, proj,
+    sb, ends, hl, hr, enb, fcb, d3, pick, put, ohf, ohe, before, grad, src,
     ls, hs, hrs, ts, trs, ps, prs, ns, nrs, rs, rrs, as_, ars, outs,
 ):
     g = lax.axis_index("grp")
@@ -315,6 +315,8 @@
         for f in range(5):
             for at in (0, HALO, HALO + FT - HW, WIDE - HW):
                 w1[f, at : at + HW, :] = blank
+            for at in (0, HW, HALO, HALO + HW, WIDE - 5 * HW, WIDE - 4 * HW, WIDE - 2 * HW, WIDE - HW):
+                w2[f, at : at + HW, :] = blank
 
         def select(links, own, shift):
             cols = lax.broadcasted_iota(jnp.int32, (links.shape[0], 256), 1)
@@ -437,14 +439,14 @@
             return jnp.concatenate([sel_mid[m, skip : n_mid - skip, :] for m in mats], 0)
 
         inner = [(HALO, HALO + FT)]
-        advance(w0, w1, mid_rows(0, (0, 1, 2)), inner, [mid], (0, 1, 2, 3, 4))
+        advance(w0, w1, mid_rows(0, (0, 1, 2)), inner, [mid], (1, 2, 3))
         one = [(mid[0] + HW, mid[1] - HW)]
-        velocity, differences = advance(w1, w0, mid_rows(HW, (0, 1, 2)), inner, one, (1, 2, 3))
+        velocity, differences = advance(w1, w2, mid_rows(HW, (0, 1, 2)), inner, one, (1, 2, 3))
         sources(0, [(2 * HW, FT - 2 * HW)], velocity, differences)
         project(0, 1)
         send_payload(0, 1)
         two = [(mid[0] + 2 * HW, mid[1] - 2 * HW)]
-        velocity, differences = differ(w0, mid_rows(2 * HW, (1, 2)), inner, two)
+        velocity, differences = differ(w2, mid_rows(2 * HW, (1, 2)), inner, two)
         sources(1, [(3 * HW, FT - 3 * HW)], velocity, differences)
         project(1, 1)
 
@@ -482,9 +484,9 @@
         def end_ranges(skip):
             return [(skip, skip + HALO), (WIDE - HALO - skip, WIDE - skip)]
 
-        advance(w0, w1, end_rows(0, (0, 1, 2)), outer, end_ranges(HW), (1, 2, 3, 0, 4))
+        advance(w0, w1, end_rows(0, (0, 1, 2)), outer, end_ranges(HW), (1, 2, 3))
         velocity, differences = advance(
-            w1, w0, end_rows(HW, (0, 1, 2)), outer, end_ranges(2 * HW), (1, 2, 3)
+            w1, w2, end_rows(HW, (0, 1, 2)), outer, end_ranges(2 * HW), (1, 2, 3)
         )
         sources(
             0,
@@ -493,15 +495,17 @@
             [[x[HW : HW + 4 * HW] for x in d] for d in differences],
         )
         project(0, 0)
+        pl.when(odd)(lambda: send_next(0, 0))
         send_payload(0, 0)
-        send_next(0, 0)
+        pl.when(even)(lambda: send_next(0, 0))
+        send_next(1, 1)
         send_payload(1, 1)
-        send_next(1, 1)
-        velocity, differences = differ(w0, end_rows(2 * HW, (1, 2)), outer, end_ranges(3 * HW))
+        velocity, differences = differ(w2, end_rows(2 * HW, (1, 2)), outer, end_ranges(3 * HW))
         sources(1, [(0, 3 * HW), (FT - 3 * HW, FT)], velocity, differences)
         project(1, 0)
+        pl.when(odd)(lambda: send_next(1, 0))
         send_payload(1, 0)
-        send_next(1, 0)
+        pl.when(even)(lambda: send_next(1, 0))
         load_targets.wait()
         inverse = hot_targets()
         for turn in range(TURNS):
@@ -509,13 +513,14 @@
             remote(
                 res.at[turn], src.at[turn, mine, :], rs.at[turn], rrs.at[turn, g], 3, s
             ).start()
-        advance(w1, w0, mid_rows(HW, (0, 1, 2)), inner, one, (0, 4))
-        advance(w1, w0, end_rows(HW, (0, 1, 2)), outer, end_ranges(2 * HW), (0, 4))
+            if turn == 0:
+                advance(w0, w1, mid_rows(0, (0, 1, 2)), inner, [mid], (0, 4))
+                advance(w0, w1, end_rows(0, (0, 1, 2)), outer, end_ranges(HW), (0, 4))
+        advance(w1, w2, mid_rows(HW, (0, 1, 2)), inner, one, (0, 4))
+        advance(w1, w2, end_rows(HW, (0, 1, 2)), outer, end_ranges(2 * HW), (0, 4))
         load_sound.wait()
         writes = [
-            pltpu.make_async_copy(w0.at[:, HALO : HALO + FT, :], fo, outs.at[0]),
-            pltpu.make_async_copy(mean, mo, outs.at[1]),
-            pltpu.make_async_copy(st, ao, outs.at[2]),
+            pltpu.make_async_copy(w2.at[:, HALO : HALO + FT, :], fo, outs.at[0]),
         ]
         for copy in writes:
             copy.start()
@@ -589,19 +594,26 @@
         load_mean.wait()
         writes = [
             pltpu.make_async_copy(w0.at[:, HALO : HALO + FT, :], fo, outs.at[0]),
-            pltpu.make_async_copy(mean, mo, outs.at[1]),
         ]
         for copy in writes:
             copy.start()
         for copy in loads:
             copy.wait()
 
-        row = lax.broadcasted_iota(jnp.int32, (EL + 128, EL), 0)
+        row = lax.broadcasted_iota(jnp.int32, (EL, EL), 0)
+        edge_row = lax.broadcasted_iota(jnp.int32, (128, 128), 0)
+        low = lax.broadcasted_iota(jnp.int32, (1, 128), 1) < 64
+
+        def edges(x):
+            return jnp.where(low, x[:, 0:128], x[:, 128:256])
+
         for f in range(6):
             link = enb[f]
-            at = link - s * EL
-            at = jnp.where(link < 0, 999, jnp.where(at < 0, at + (EL + 128), at))
+            at = jnp.where(link < 0, 999, link - s * EL)
             ohf[f] = jnp.where(row == at, F32(1.0), F32(0.0)).astype(BF16)
+            at = edges(at)
+            at = jnp.where(at < 0, at + 128, jnp.where(at < EL, 999, at - EL))
+            ohe[f] = jnp.where(edge_row == at, F32(1.0), F32(0.0)).astype(BF16)
         node = lax.broadcasted_iota(jnp.int32, (NP, EL), 0)
         faces_on = jnp.zeros((NP, EL), F32)
         for f in range(6):
@@ -613,6 +625,36 @@
             for v in range(4):
                 hi, lo = halves(st[v])
                 grad[v] = dot(d3[...], jnp.concatenate([hi, lo, hi], 0))
+
+            def jumps(facing, hot, code):
+                remotes = []
+                for f in range(6):
+                    stacked = jnp.concatenate(
+                        [facing[v][16 * f : 16 * f + 16] for v in range(4)], 0
+                    )
+                    remotes.append(dot(stacked, hot[f]))
+                out = []
+                for v in range(4):
+                    turned = [
+                        jnp.where(
+                            code(f) == r, remotes[f][16 * v : 16 * v + 16], F32(0.0)
+                        ).astype(BF16)
+                        for r in range(4)
+                        for f in range(6)
+                    ]
+                    out.append(dot(put[...], jnp.concatenate(turned, 0)))
+                return out
+
+            facing = [
+                dot(pick[...], sb[turn, NP * v : NP * (v + 1), :]).astype(BF16) for v in range(4)
+            ]
+            within = jumps(facing, ohf, lambda f: fcb[f])
+            for v in range(4):
+                if v == 0:
+                    linear = grad[1, 0:64] + grad[2, 64:128] + grad[3, 128:192]
+                else:
+                    linear = grad[0, 64 * (v - 1) : 64 * v]
+                before[v] = st[v] + 0.08 * (1.5 * (within[v] - faces_on * st[v]) - linear)
             sends.wait_recv()
             sends.wait_send()
             after, before_ = hr[turn].astype(F32), hl[turn].astype(F32)
@@ -627,31 +669,14 @@
                 ],
                 0,
             ).astype(BF16)
-            facing = []
+            facing = [
+                dot(pick[...], beside[NP * v : NP * (v + 1)]).astype(BF16) for v in range(4)
+            ]
+            across = jumps(facing, ohe, lambda f: edges(fcb[f]))
             for v in range(4):
-                rows = slice(NP * v, NP * (v + 1))
-                wide = jnp.concatenate([sb[turn, rows, :], beside[rows]], 1)
-                facing.append(dot(pick[...], wide).astype(BF16))
-            remotes = []
-            for f in range(6):
-                stacked = jnp.concatenate([facing[v][16 * f : 16 * f + 16] for v in range(4)], 0)
-                remotes.append(dot(stacked, ohf[f]))
-            before = []
-            for v in range(4):
-                turned = []
-                for r in range(4):
-                    for f in range(6):
-                        turned.append(
-                            jnp.where(
-                                fcb[f] == r, remotes[f][16 * v : 16 * v + 16], F32(0.0)
-                            ).astype(BF16)
-                        )
-                jump = dot(put[...], jnp.concatenate(turned, 0)) - faces_on * st[v]
-                if v == 0:
-                    linear = grad[1, 0:64] + grad[2, 64:128] + grad[3, 128:192]
-                else:
-                    linear = grad[0, 64 * (v - 1) : 64 * v]
-                before.append(st[v] + 0.08 * (1.5 * jump - linear))
+                added = 0.08 * 1.5 * across[v]
+                before[v, :, 0:128] += jnp.where(low, added, F32(0.0))
+                before[v, :, 128:256] += jnp.where(low, F32(0.0), added)
             for w in range(3):
                 rows = slice(SHARE * w, SHARE * w + SHARE)
                 remote(
@@ -665,11 +690,8 @@
                 st[v] = before[v] - 0.08 * convect
             if turn == 0:
                 sends = send_state(1)
-        write = pltpu.make_async_copy(st, ao, outs.at[2])
-        write.start()
         for copy in writes:
             copy.wait()
-        write.wait()
 
 
 def store(a, b, c, x, y, z, sems):
@@ -687,6 +709,7 @@
     n_sfc = lax.axis_size("sfc")
     hbm = pl.BlockSpec(memory_space=pltpu.MemorySpace.HBM)
     any_space = pl.BlockSpec(memory_space=pl.ANY)
+    vmem = pl.BlockSpec(memory_space=pltpu.MemorySpace.VMEM)
     dma = pltpu.SemaphoreType.DMA
     outs = pl.pallas_call(
         functools.partial(kernel, n_sfc),
@@ -696,15 +719,15 @@
             jax.ShapeDtypeStruct((4, NP, EL), F32),
         ),
         in_specs=[hbm] * 12,
-        out_specs=(any_space,) * 3,
+        out_specs=(any_space, vmem, vmem),
         scratch_shapes=[
+            pltpu.VMEM((5, WIDE, CELLS), F32),
             pltpu.VMEM((5, WIDE, CELLS), F32),
             pltpu.VMEM((5, WIDE, CELLS), F32),
             pltpu.VMEM((WIDE, CELLS), F32),
             pltpu.VMEM((2, 6, HALO, CELLS), BF16),
             pltpu.VMEM((2, 6, HALO, CELLS), BF16),
             pltpu.VMEM((8, 256 + FT), jnp.int32),
-            pltpu.VMEM((3, FT, CELLS), F32),
             pltpu.VMEM((3, FT - 2 * HW, 256), BF16),
             pltpu.VMEM((3, 10 * HW, 256), BF16),
             pltpu.VMEM((TURNS, 2, 6, 128, 256), BF16),
@@ -718,7 +741,6 @@
             pltpu.VMEM((SHARE, EL), F32),
             pltpu.VMEM((TURNS, SHARE, EL), BF16),
             pltpu.VMEM((NP, CELLS), F32),
-            pltpu.VMEM((4, NP, EL), F32),
             pltpu.VMEM((TURNS, 4 * NP, EL), BF16),
             pltpu.VMEM((TURNS, 2, 32, 128), BF16),
             pltpu.VMEM((TURNS, 32, 128), BF16),
@@ -728,7 +750,9 @@
             pltpu.VMEM((192, 192), BF16),
             pltpu.VMEM((96, NP), BF16),
             pltpu.VMEM((NP, 384), BF16),
-            pltpu.VMEM((6, EL + 128, EL), BF16),
+            pltpu.VMEM((6, EL, EL), BF16),
+            pltpu.VMEM((6, 128, 128), BF16),
+            pltpu.VMEM((4, NP, EL), F32),
             pltpu.VMEM((4, 192, EL), F32),
             pltpu.VMEM((TURNS, 6 * NP, EL), BF16),
             dma((8,)),
@@ -738,7 +762,7 @@
             dma((TURNS, 2)), dma((TURNS, 2)),
             dma((TURNS,)), dma((TURNS, 3)),
             dma((TURNS, 2)), dma((TURNS, 2)),
-            dma((3,)),
+            dma((1,)),
         ],
         compiler_params=pltpu.CompilerParams(
             collective_id=0, has_side_effects=True, vmem_limit_bytes=48 * 1024 * 1024

time: 25.1 us -> 24.6 us (0.980)
  Pallas kernels: 24.3 us -> 23.8 us
    pallas_call x1, Pallas kernels: 23.3 us -> 22.8 us  [body(): pl.pallas_call(functools.partial(kernel, n_sfc), out_shape=(jax.ShapeDtyp...]
where the time goes in v4:
time: 24.6 us; the launch traced here: 24.5 us
  Pallas kernels  23.8 us (97%)
  between operations  0.64 us (3%)
    pallas_call x1, Pallas kernels, body(): pl.pallas_call(functools.partial(kernel, n_sfc), out_shape=(jax.ShapeDtyp...  22.8 us
    pallas_call x1, Pallas kernels, body(): pl.pallas_call(store, out_shape=tuple((jax.ShapeDtypeStruct(o.shape, o.dt...  1.08 us

profile of v4, /device:TPU:56, one launch (start us, length us, event | category | flops | bytes accessed | tf_op | source)
XLA Modules:
  0.0 24.5 jit_solution(8297106157719011207)
XLA Ops:
  0.6 22.8 %shard_map.139 = (f32[5,256,128]{2,1,0:T(8,128)S(1)}, f32[3,256,128]{2,1,0:T(8,128)S(1)}, f32[4,64,256]{2,1,0:T(8,128)S(1)}) custom-call(f32[5,256,128]{2,1,0:T(8,128)} %bitcast.10, f32[3,256,128]{2,1,0:T(8,128)} %bitcast.11, f32[256,128]{1,0:T(8,128)} %bitcast.13, s32[4,256]{1,0:T(4,128)} %bitcast.16, s32[1,256]{1,0:T(1,128)} %tt.1, f32[64,128]{1,0:T(8,128)} %pj.1, ...), custom_call_target="tpu_custom_call" | custom-call | tf_op jit(solution)/shard_map/pallas_call | solution.py:714
  23.4 1.1 %shard_map.140 = (f32[5,256,128]{2,1,0:T(8,128)}, f32[3,256,128]{2,1,0:T(8,128)}, f32[4,64,256]{2,1,0:T(8,128)}) custom-call(f32[5,256,128]{2,1,0:T(8,128)S(1)} %get-tuple-element.9.a, f32[3,256,128]{2,1,0:T(8,128)S(1)} %get-tuple-element.10.b, f32[4,64,256]{2,1,0:T(8,128)S(1)} %get-tuple-element.11.c), custom_call_target="tpu_custom_call" | custom-call | tf_op jit(solution)/shard_map/pallas_call | solution.py:777
